TPU v7x, 128 devices: a whole 4x4x4 slice. The times are simulated.
128 devices in a mesh: row: 8 (over z, x_lo), col: 16 (over x_hi, y, core).
Axes of the slice: x: 4 (x_hi: 2, x_lo: 2; x = x_hi * 2 + x_lo), y: 4, z: 4, core: 2. Of those that a mesh axis runs over, the one named last changes fastest.
Arguments:
- positions: float32 [3, 16, 16, 16, 128], P(None, 'row', 'col'), may hold values from 0.5 to 7.5
- torques: float32 [3, 16, 16, 16, 128], P(None, 'row', 'col'), may hold values from -6 to 6
- counts: int32 [16, 16, 16], P('row', 'col'), may hold values from 42 to 128
- neighbour_flags: int32 [6, 16, 16, 16], P(None, 'row', 'col'), may hold values 0 or 1
Outputs:
- moved_positions: float32 [3, 16, 16, 16, 128], P(None, 'row', 'col')
- spin: float32 [3, 16, 16, 16, 128], P(None, 'row', 'col')
Inputs may be any that keep to these rules, and one draw needn't show every extreme that they name: `counts`: number of occupied slots of each cell block; slots at or past it hold no particle. `neighbour_flags`: entry f of a block is 1 where its neighbour at the f-th face offset (+x, -x, +y, -y, +z, -z) acts on it, else 0.
All inputs are finite; a program needn't handle non-finite values.
Results may differ from a plain program's by a relative error of at most 0.0003.
Values sent between devices are 32-bit elements; how exact they have to be, the bound alone decides.
A program may use at most 64 MiB of HBM per device.

v0:
```python
import math

import jax
import jax.numpy as jnp
from jax import lax
from jax.sharding import PartitionSpec as P

GRID = 128
CELL = 8
STEPS = 3


highest = lax.Precision.HIGHEST
step_pace = 0.06
drift_gain = 1.0
couple_gain = 0.5
bin_rate = 1.0
face_moves = ((0, 1.0), (0, -1.0), (1, 1.0), (1, -1.0), (2, 1.0), (2, -1.0))


def with_halo(block, sides, width):
    for axis, dim in sides:
        count = lax.axis_size(axis)
        forward = [(i, i + 1) for i in range(count - 1)]
        forward.append((count - 1, 0))
        backward = [(target, source) for source, target in forward]
        low = lax.ppermute(
            lax.slice_in_dim(block, block.shape[dim] - width, None, axis=dim), axis, forward
        )
        high = lax.ppermute(lax.slice_in_dim(block, 0, width, axis=dim), axis, backward)
        block = jnp.concatenate([low, block, high], axis=dim)
    return block


def cross_product(left_vec, right_vec):
    return jnp.stack(
        [
            left_vec[1] * right_vec[2] - left_vec[2] * right_vec[1],
            left_vec[2] * right_vec[0] - left_vec[0] * right_vec[2],
            left_vec[0] * right_vec[1] - left_vec[1] * right_vec[0],
        ]
    )


def make_loads(places, torque, filled):
    return jnp.concatenate(
        [torque * filled, cross_product(torque, places) * filled, filled[None]], 0
    )


def pair_totals(near_places, far_places, far_loads, offset_vec):
    separation = (
        near_places[:, :, :, None] - far_places[:, :, None, :] - offset_vec[:, None, None, None]
    )
    weights = jnp.exp(-jnp.sum(separation * separation, axis=0) * (2.0 / (CELL * CELL)))
    return jnp.einsum("nij,qnj->qni", weights, far_loads, precision=highest)


def neighbours(extended):
    centre = extended[:, 1:-1, 1:-1]
    return [
        centre,
        extended[:, 2:, 1:-1],
        extended[:, :-2, 1:-1],
        extended[:, 1:-1, 2:],
        extended[:, 1:-1, :-2],
        jnp.roll(centre, -1, axis=3),
        jnp.roll(centre, 1, axis=3),
    ]


def near_field(places, torque, filled, face_flags, far_place_list, far_load_list):
    layout = places.shape
    cell_count = layout[1] * layout[2] * layout[3]

    def flatten(values):
        return values.reshape(values.shape[0], cell_count, layout[4])

    drives = jnp.zeros(layout, jnp.float32)
    twists = jnp.zeros(layout, jnp.float32)
    weight_total = jnp.zeros(layout[1:], jnp.float32)
    for face_id in range(7):
        if face_id == 0:
            offset_vec = jnp.zeros((3,), jnp.float32)
            face_gate = jnp.ones(layout[1:4] + (1,), jnp.float32)
        else:
            axis_id, face_sign = face_moves[face_id - 1]
            offset_vec = jnp.zeros((3,), jnp.float32).at[axis_id].set(face_sign * CELL)
            face_gate = face_flags[face_id - 1].astype(jnp.float32)[..., None]
        totals = pair_totals(
            flatten(places),
            flatten(far_place_list[face_id]),
            flatten(far_load_list[face_id]),
            offset_vec,
        )
        totals = totals.reshape((7,) + layout[1:])
        lever = places - offset_vec[:, None, None, None, None]
        drives = drives + face_gate * (cross_product(totals[0:3], lever) - totals[3:6])
        twists = twists + face_gate * totals[0:3]
        weight_total = weight_total + face_gate * totals[6]
    velocity = drift_gain / layout[4] * drives * filled
    spin_near = (torque + couple_gain / layout[4] * (twists - weight_total * torque)) * filled
    return (velocity, spin_near)


def bin_weights(coordinate):
    centres = jnp.arange(CELL, dtype=jnp.float32) + 0.5
    separation = coordinate[..., None] - centres
    return jnp.exp(-separation * separation * bin_rate)


def signed_wave(values):
    return jnp.where(values < GRID // 2, values, values - GRID).astype(jnp.float32)


def stokes(spectrum, wave_x, wave_y, wave_z):
    wave_square = wave_x * wave_x + wave_y * wave_y + wave_z * wave_z
    damping = 0.25 * jnp.exp(-wave_square * (math.pi / GRID) ** 2)
    along = (wave_x * spectrum[0] + wave_y * spectrum[1] + wave_z * spectrum[2]) / jnp.maximum(
        wave_square, 1.0
    )
    return jnp.stack(
        [
            damping * (spectrum[0] - wave_x * along),
            damping * (spectrum[1] - wave_y * along),
            damping * (spectrum[2] - wave_z * along),
        ]
    )


def dft_tables(length):
    counter = jnp.arange(length, dtype=jnp.int32)
    phase = counter[:, None] * counter[None, :] % length
    angle = phase.astype(jnp.float32) * (2.0 * math.pi / length)
    return (jnp.cos(angle), jnp.sin(angle))


def spectral_forward(pieces, form, cosine, sine_tab):
    real_out = jnp.einsum(form, pieces[0], cosine, precision=highest) + jnp.einsum(
        form, pieces[1], sine_tab, precision=highest
    )
    imag_out = jnp.einsum(form, pieces[1], cosine, precision=highest) - jnp.einsum(
        form, pieces[0], sine_tab, precision=highest
    )
    return jnp.stack([real_out, imag_out])


def spectral_inverse(pieces, form, cosine, sine_tab):
    real_out = jnp.einsum(form, pieces[0], cosine, precision=highest) - jnp.einsum(
        form, pieces[1], sine_tab, precision=highest
    )
    imag_out = jnp.einsum(form, pieces[1], cosine, precision=highest) + jnp.einsum(
        form, pieces[0], sine_tab, precision=highest
    )
    return jnp.stack([real_out, imag_out])


def apply_stokes(spectrum, wave_x, wave_y, wave_z):
    return jnp.stack(
        [stokes(spectrum[0], wave_x, wave_y, wave_z), stokes(spectrum[1], wave_x, wave_y, wave_z)]
    )


def solve_far(grid_field):
    cosine, sine_tab = dft_tables(GRID)
    real_part = jnp.einsum("cxyz,zk->ckxy", grid_field, cosine, precision=highest)
    imag_part = -jnp.einsum("cxyz,zk->ckxy", grid_field, sine_tab, precision=highest)
    spectrum = jnp.stack([real_part, imag_part])
    pencil = spectral_forward(
        lax.all_to_all(spectrum, "col", split_axis=2, concat_axis=4, tiled=True),
        "ckxy,yl->clkx",
        cosine,
        sine_tab,
    )
    pencil = spectral_forward(
        lax.all_to_all(pencil, "row", split_axis=2, concat_axis=4, tiled=True),
        "clkx,xm->clkm",
        cosine,
        sine_tab,
    )
    ky_count = pencil.shape[2]
    kz_count = pencil.shape[3]
    wave_y = signed_wave(lax.axis_index("row") * ky_count + jnp.arange(ky_count, dtype=jnp.int32))[
        :, None, None
    ]
    wave_z = signed_wave(lax.axis_index("col") * kz_count + jnp.arange(kz_count, dtype=jnp.int32))[
        None, :, None
    ]
    wave_x = signed_wave(jnp.arange(GRID, dtype=jnp.int32))[None, None, :]
    pencil = apply_stokes(pencil, wave_x, wave_y, wave_z)
    pencil = spectral_inverse(pencil, "clkm,mx->clkx", cosine, sine_tab)
    pencil = spectral_inverse(
        lax.all_to_all(pencil, "row", split_axis=4, concat_axis=2, tiled=True),
        "clkx,ly->ckxy",
        cosine,
        sine_tab,
    )
    pieces = lax.all_to_all(pencil, "col", split_axis=4, concat_axis=2, tiled=True)
    summed = jnp.einsum("ckxy,kz->cxyz", pieces[0], cosine, precision=highest) - jnp.einsum(
        "ckxy,kz->cxyz", pieces[1], sine_tab, precision=highest
    )
    return summed * (1.0 / GRID) ** 3


def far_field(places, torque, filled):
    cells_x, cells_y, cells_z, slot_count = (
        places.shape[1],
        places.shape[2],
        places.shape[3],
        places.shape[4],
    )
    cell_count = cells_x * cells_y * cells_z
    flat_places = places.reshape(3, cell_count, slot_count)
    weight_x = bin_weights(flat_places[0])
    weight_y = bin_weights(flat_places[1])
    weight_z = bin_weights(flat_places[2])
    planar = weight_x[:, :, :, None] * weight_y[:, :, None, :]
    lifted = (torque * filled).reshape(3, cell_count, slot_count)[:, :, :, None] * weight_z[None]
    cubes = jnp.einsum("niab,qnic->qnabc", planar, lifted, precision=highest)
    grid_field = (
        cubes.reshape(3, cells_x, cells_y, cells_z, CELL, CELL, CELL)
        .transpose(0, 1, 4, 2, 5, 3, 6)
        .reshape(3, cells_x * CELL, cells_y * CELL, cells_z * CELL)
    )
    far_grid = solve_far(grid_field)
    cubes = (
        far_grid.reshape(3, cells_x, CELL, cells_y, CELL, cells_z, CELL)
        .transpose(0, 1, 3, 5, 2, 4, 6)
        .reshape(3, cell_count, CELL, CELL, CELL)
    )
    partial_sum = jnp.einsum("qnabc,niab->qnic", cubes, planar, precision=highest)
    return jnp.sum(partial_sum * weight_z[None], axis=3).reshape(
        3, cells_x, cells_y, cells_z, slot_count
    )


def shards(positions, torques, counts, neighbour_flags):
    slot_count = positions.shape[4]
    filled = (jnp.arange(slot_count, dtype=jnp.int32) < counts[..., None]).astype(jnp.float32)
    places = positions
    spin_near = jnp.zeros(positions.shape, jnp.float32)
    for step_id in range(STEPS):
        loads = make_loads(places, torques, filled)
        state_rim = with_halo(jnp.concatenate([places, loads], 0), (("row", 1), ("col", 2)), 1)
        place_rim = state_rim[0:3]
        load_rim = state_rim[3:10]
        velocity, spin_near = near_field(
            places, torques, filled, neighbour_flags, neighbours(place_rim), neighbours(load_rim)
        )
        places = places + step_pace * CELL * velocity
    far_spin = far_field(places, torques, filled)
    return (places, spin_near + far_spin * filled)


def solution(mesh):
    in_specs = (
        P(None, "row", "col", None, None),
        P(None, "row", "col", None, None),
        P("row", "col", None),
        P(None, "row", "col", None),
    )
    out_specs = (P(None, "row", "col", None, None), P(None, "row", "col", None, None))
    return jax.shard_map(shards, mesh=mesh, in_specs=in_specs, out_specs=out_specs, check_vma=False)
```

profile of v0, /device:TPU:1, one launch (start us, length us, event | category | flops | bytes accessed | tf_op | source)
XLA Modules:
  0.0 325.1 jit_solution(7276185580779375041)
XLA Ops:
  4.7 5.6 %collective-permute-start = (f32[10,1,1,16,128]{4,3,2,1,0:T(8,128)S(1)}, f32[10,1,1,16,128]{4,3,2,1,0:T(8,128)S(1)}, u32[]{:S(2)}, u32[]{:S(2)}) collective-permute-start(f32[10,1,1,16,128]{4,3,2,1,0:T(8,128)S(1)} %get-tuple-element.221), channel_id=1, source_target_pairs={{16,0},{32,16},{48,32},{64,48},{80,64},{96,80},{112,96},{0,112},{1... | collective-permute-start | bytes 245768 | tf_op jit(solution)/shard_map/ppermute | solution.py:30
  15.7 3.4 %collective-permute-start.3 = (f32[10,4,1,16,128]{4,3,2,1,0:T(8,128)S(1)}, f32[10,4,1,16,128]{4,3,2,1,0:T(8,128)S(1)}, u32[]{:S(2)}, u32[]{:S(2)}) collective-permute-start(f32[10,4,1,16,128]{4,3,2,1,0:T(8,128)S(1)} %fusion.215), channel_id=1, source_target_pairs={{0,1},{1,2},{2,3},{3,4},{4,5},{5,6},{6,7},{7,8},{8,9},{9,10},{10,1... | collective-permute-start | bytes 983048 | tf_op jit(solution)/shard_map/ppermute | solution.py:27
  19.4 3.7 %collective-permute-done.3 = f32[10,4,1,16,128]{4,3,2,1,0:T(8,128)S(1)} collective-permute-done((f32[10,4,1,16,128]{4,3,2,1,0:T(8,128)S(1)}, f32[10,4,1,16,128]{4,3,2,1,0:T(8,128)S(1)}, u32[]{:S(2)}, u32[]{:S(2)}) %collective-permute-start.3) | collective-permute-done | bytes 327712 | tf_op jit(solution)/shard_map/ppermute | solution.py:27
  23.1 2.8 collective-permute-done.2
  25.9 12.3 %multiply_reduce_fusion.14 = (f32[32,128,128]{2,1,0:T(8,128)S(1)}, f32[32,128,128]{2,1,0:T(8,128)S(1)}, f32[32,128,128]{2,1,0:T(8,128)S(1)}, f32[32,128,128]{2,1...) fusion(f32[3]{0:T(128)S(1)} %copy-done.44, ...), kind=kLoop, calls=%fused_computation.14 | loop fusion | flops 38797312 | bytes 15024200 | tf_op jit(solution)/shard_map/reduce_sum | solution.py:55
  38.2 3.4 %fusion.122 = f32[7,32,128]{2,0,1:T(8,128)S(1)} fusion(f32[7,32,128]{2,0,1:T(8,128)S(1)} %bitcast.612, f32[32,128,128]{2,1,0:T(8,128)S(1)} %get-tuple-element.185), kind=kOutput, calls=%fused_computation.144 | convolution fusion | flops 45088768 | bytes 2326528 | tf_op jit(solution)/shard_map/nij,qnj->qni/dot_general | solution.py:56
  41.7 3.4 %fusion.134 = f32[7,32,128]{2,0,1:T(8,128)S(1)} fusion(f32[7,32,128]{2,0,1:T(8,128)S(1)} %bitcast.607, f32[32,128,128]{2,1,0:T(8,128)S(1)} %get-tuple-element.184), kind=kOutput, calls=%fused_computation.148 | convolution fusion | flops 45088768 | bytes 2326528 | tf_op jit(solution)/shard_map/nij,qnj->qni/dot_general | solution.py:56
  45.2 3.4 %fusion.125 = f32[7,32,128]{2,0,1:T(8,128)S(1)} fusion(f32[7,32,128]{2,0,1:T(8,128)S(1)} %bitcast.614, f32[32,128,128]{2,1,0:T(8,128)S(1)} %get-tuple-element.186), kind=kOutput, calls=%fused_computation.145 | convolution fusion | flops 45088768 | bytes 2326528 | tf_op jit(solution)/shard_map/nij,qnj->qni/dot_general | solution.py:56
  48.8 3.4 %fusion.128 = f32[7,32,128]{2,0,1:T(8,128)S(1)} fusion(f32[7,32,128]{2,0,1:T(8,128)S(1)} %bitcast.615, f32[32,128,128]{2,1,0:T(8,128)S(1)} %get-tuple-element.187), kind=kOutput, calls=%fused_computation.146 | convolution fusion | flops 45088768 | bytes 2326528 | tf_op jit(solution)/shard_map/nij,qnj->qni/dot_general | solution.py:56
  52.2 3.8 %fusion.131 = f32[7,32,128]{2,0,1:T(8,128)S(1)} fusion(f32[7,32,128]{2,0,1:T(8,128)S(1)} %bitcast.603, f32[32,128,128]{2,1,0:T(8,128)S(1)} %get-tuple-element.188), kind=kOutput, calls=%fused_computation.147 | convolution fusion | flops 45088768 | bytes 2326528 | tf_op jit(solution)/shard_map/nij,qnj->qni/dot_general | solution.py:56
  56.1 3.4 %fusion.119 = f32[7,32,128]{2,0,1:T(8,128)S(1)} fusion(f32[7,32,128]{2,0,1:T(8,128)S(1)} %bitcast.609, f32[32,128,128]{2,1,0:T(8,128)S(1)} %get-tuple-element.190), kind=kOutput, calls=%fused_computation.143 | convolution fusion | flops 45088768 | bytes 2326528 | tf_op jit(solution)/shard_map/nij,qnj->qni/dot_general | solution.py:56
  59.5 3.4 %fusion.116 = f32[7,32,128]{2,0,1:T(8,128)S(1)} fusion(f32[32,128,128]{2,1,0:T(8,128)S(1)} %get-tuple-element.189, f32[1,32,128]{2,0,1:T(1,128)S(1)} %compare_convert_fusion, f32[3,32,128]{2,0,1:T(4,128)S(1)} %bitcast.598, f32[3,32,128]{2,0,1:T(4,128)S(1)} %maximum_multiply_fusion), kind=kOutput, calls=%fused_computation.142 | convolution fusion | flops 45146112 | bytes 2326528 | tf_op jit(solution)/shard_map/nij,qnj->qni/dot_general | solution.py:56
  63.8 2.5 collective-permute-start.4
  67.8 3.9 %collective-permute-done.5 = f32[10,1,1,16,128]{4,3,2,1,0:T(8,128)S(1)} collective-permute-done((f32[10,1,1,16,128]{4,3,2,1,0:T(8,128)S(1)}, f32[10,1,1,16,128]{4,3,2,1,0:T(8,128)S(1)}, u32[]{:S(2)}, u32[]{:S(2)}) %collective-permute-start.5) | collective-permute-done | bytes 81952 | tf_op jit(solution)/shard_map/ppermute | solution.py:27
  71.7 1.7 collective-permute-start.7
  73.4 2.1 collective-permute-start.6
  75.8 1.6 collective-permute-done.7
  77.4 2.5 collective-permute-done.6
  79.9 12.3 %multiply_reduce_fusion.7 = (f32[32,128,128]{2,1,0:T(8,128)S(1)}, f32[32,128,128]{2,1,0:T(8,128)S(1)}, f32[32,128,128]{2,1,0:T(8,128)S(1)}, f32[32,128,128]{2,1,...) fusion(f32[3,32,128]{2,1,0:T(8,128)S(1)} %bitcast.652, ...), kind=kLoop, calls=%fused_computation.7 | loop fusion | flops 38797312 | bytes 15024200 | tf_op jit(solution)/shard_map/reduce_sum | solution.py:55
  92.2 3.4 %fusion.143 = f32[7,32,128]{2,0,1:T(8,128)S(1)} fusion(f32[7,32,128]{2,0,1:T(8,128)S(1)} %bitcast.613, f32[32,128,128]{2,1,0:T(8,128)S(1)} %get-tuple-element.178), kind=kOutput, calls=%fused_computation.151 | convolution fusion | flops 45088768 | bytes 2326528 | tf_op jit(solution)/shard_map/nij,qnj->qni/dot_general | solution.py:56
  95.7 3.4 %fusion.155 = f32[7,32,128]{2,0,1:T(8,128)S(1)} fusion(f32[7,32,128]{2,0,1:T(8,128)S(1)} %bitcast.608, f32[32,128,128]{2,1,0:T(8,128)S(1)} %get-tuple-element.177), kind=kOutput, calls=%fused_computation.155 | convolution fusion | flops 45088768 | bytes 2326528 | tf_op jit(solution)/shard_map/nij,qnj->qni/dot_general | solution.py:56
  99.2 3.4 %fusion.146 = f32[7,32,128]{2,0,1:T(8,128)S(1)} fusion(f32[7,32,128]{2,0,1:T(8,128)S(1)} %bitcast.616, f32[32,128,128]{2,1,0:T(8,128)S(1)} %get-tuple-element.179), kind=kOutput, calls=%fused_computation.152 | convolution fusion | flops 45088768 | bytes 2326528 | tf_op jit(solution)/shard_map/nij,qnj->qni/dot_general | solution.py:56
  102.7 3.4 %fusion.149 = f32[7,32,128]{2,0,1:T(8,128)S(1)} fusion(f32[7,32,128]{2,0,1:T(8,128)S(1)} %bitcast.617, f32[32,128,128]{2,1,0:T(8,128)S(1)} %get-tuple-element.180), kind=kOutput, calls=%fused_computation.153 | convolution fusion | flops 45088768 | bytes 2326528 | tf_op jit(solution)/shard_map/nij,qnj->qni/dot_general | solution.py:56
  106.2 3.6 %fusion.152 = f32[7,32,128]{2,0,1:T(8,128)S(1)} fusion(f32[7,32,128]{2,0,1:T(8,128)S(1)} %bitcast.604, f32[32,128,128]{2,1,0:T(8,128)S(1)} %get-tuple-element.181), kind=kOutput, calls=%fused_computation.154 | convolution fusion | flops 45088768 | bytes 2326528 | tf_op jit(solution)/shard_map/nij,qnj->qni/dot_general | solution.py:56
  109.8 3.4 %fusion.140 = f32[7,32,128]{2,0,1:T(8,128)S(1)} fusion(f32[7,32,128]{2,0,1:T(8,128)S(1)} %bitcast.610, f32[32,128,128]{2,1,0:T(8,128)S(1)} %get-tuple-element.183), kind=kOutput, calls=%fused_computation.150 | convolution fusion | flops 45088768 | bytes 2326528 | tf_op jit(solution)/shard_map/nij,qnj->qni/dot_general | solution.py:56
  113.3 3.4 %fusion.137 = f32[7,32,128]{2,0,1:T(8,128)S(1)} fusion(f32[32,128,128]{2,1,0:T(8,128)S(1)} %get-tuple-element.182, f32[1,32,128]{2,0,1:T(1,128)S(1)} %compare_convert_fusion, f32[3,32,128]{2,0,1:T(4,128)S(1)} %bitcast.599, f32[3,32,128]{2,0,1:T(4,128)S(1)} %maximum_multiply_fusion.1), kind=kOutput, calls=%fused_computation.149 | convolution fusion | flops 45146112 | bytes 2326528 | tf_op jit(solution)/shard_map/nij,qnj->qni/dot_general | solution.py:56
  117.6 1.5 collective-permute-start.9
  119.1 1.8 collective-permute-done.8
  120.9 2.2 collective-permute-done.9
  124.4 5.7 %collective-permute-start.10 = (f32[10,4,1,16,128]{4,3,2,1,0:T(8,128)S(1)}, f32[10,4,1,16,128]{4,3,2,1,0:T(8,128)S(1)}, u32[]{:S(2)}, u32[]{:S(2)}) collective-permute-start(f32[10,4,1,16,128]{4,3,2,1,0:T(8,128)S(1)} %fusion.219), channel_id=1, source_target_pairs={{1,0},{2,1},{3,2},{4,3},{5,4},{6,5},{7,6},{8,7},{9,8},{10,9},{11,1... | collective-permute-start | bytes 983048 | tf_op jit(solution)/shard_map/ppermute | solution.py:30
  131.3 12.5 %multiply_reduce_fusion = (f32[32,128,128]{2,1,0:T(8,128)S(1)}, f32[32,128,128]{2,1,0:T(8,128)S(1)}, f32[32,128,128]{2,1,0:T(8,128)S(1)}, f32[32,128,128]{2,1,0:...) fusion(f32[3,32,128]{2,1,0:T(8,128)S(1)} %bitcast.650, ...), kind=kLoop, calls=%fused_computation | loop fusion | flops 38797312 | bytes 15024200 | tf_op jit(solution)/shard_map/reduce_sum | solution.py:55
  143.8 3.4 %fusion.158 = f32[7,32,128]{2,0,1:T(8,128)S(1)} fusion(f32[32,128,128]{2,1,0:T(8,128)S(1)} %get-tuple-element.175, f32[1,32,128]{2,0,1:T(1,128)S(1)} %compare_convert_fusion, f32[3,32,128]{2,0,1:T(4,128)S(1)} %bitcast.600, f32[3,32,128]{2,0,1:T(4,128)S(1)} %maximum_multiply_fusion.2), kind=kOutput, calls=%fused_computation.156 | convolution fusion | flops 45146112 | bytes 2326528 | tf_op jit(solution)/shard_map/nij,qnj->qni/dot_general | solution.py:56
  148.5 3.4 %fusion.164 = f32[7,32,128]{2,0,1:T(8,128)S(1)} fusion(f32[7,32,128]{2,0,1:T(8,128)S(1)} %bitcast.611, f32[32,128,128]{2,1,0:T(8,128)S(1)} %get-tuple-element.171), kind=kOutput, calls=%fused_computation.158 | convolution fusion | flops 45088768 | bytes 2326528 | tf_op jit(solution)/shard_map/nij,qnj->qni/dot_general | solution.py:56
  153.2 3.4 %fusion.176 = f32[7,32,128]{2,0,1:T(8,128)S(1)} fusion(f32[7,32,128]{2,0,1:T(8,128)S(1)} %bitcast.605, f32[32,128,128]{2,1,0:T(8,128)S(1)} %get-tuple-element.170), kind=kOutput, calls=%fused_computation.162 | convolution fusion | flops 45088768 | bytes 2326528 | tf_op jit(solution)/shard_map/nij,qnj->qni/dot_general | solution.py:56
  157.9 3.4 %fusion.167 = f32[7,32,128]{2,0,1:T(8,128)S(1)} fusion(f32[7,32,128]{2,0,1:T(8,128)S(1)} %bitcast.618, f32[32,128,128]{2,1,0:T(8,128)S(1)} %get-tuple-element.172), kind=kOutput, calls=%fused_computation.159 | convolution fusion | flops 45088768 | bytes 2326528 | tf_op jit(solution)/shard_map/nij,qnj->qni/dot_general | solution.py:56
  162.7 3.5 %fusion.170 = f32[7,32,128]{2,0,1:T(8,128)S(1)} fusion(f32[7,32,128]{2,0,1:T(8,128)S(1)} %bitcast.619, f32[32,128,128]{2,1,0:T(8,128)S(1)} %get-tuple-element.173), kind=kOutput, calls=%fused_computation.160 | convolution fusion | flops 45088768 | bytes 2326528 | tf_op jit(solution)/shard_map/nij,qnj->qni/dot_general | solution.py:56
  167.5 3.4 %fusion.173 = f32[7,32,128]{2,0,1:T(8,128)S(1)} fusion(f32[7,32,128]{2,0,1:T(8,128)S(1)} %bitcast.602, f32[32,128,128]{2,1,0:T(8,128)S(1)} %get-tuple-element.174), kind=kOutput, calls=%fused_computation.161 | convolution fusion | flops 45088768 | bytes 2326528 | tf_op jit(solution)/shard_map/nij,qnj->qni/dot_general | solution.py:56
  172.2 3.4 %fusion.161 = f32[7,32,128]{2,0,1:T(8,128)S(1)} fusion(f32[7,32,128]{2,0,1:T(8,128)S(1)} %bitcast.606, f32[32,128,128]{2,1,0:T(8,128)S(1)} %get-tuple-element.176), kind=kOutput, calls=%fused_computation.157 | convolution fusion | flops 45088768 | bytes 2326528 | tf_op jit(solution)/shard_map/nij,qnj->qni/dot_general | solution.py:56
  177.8 14.3 %fusion.180 = f32[32,3,8,8,8]{4,2,3,1,0:T(8,128)S(1)} fusion(f32[32,128,8]{1,2,0:T(8,128)S(1)} %get-tuple-element.435, f32[32,128,8]{1,2,0:T(8,128)S(1)} %get-tuple-element.436, f32[32,128,8]{1,2,0:T(8,128)S(1)} %get-tuple-element.434, f32[3,32,128]{2,0,1:T(4,128)S(1)} %bitcast.601), kind=kOutput, calls=%fused_computation.164 | convolution fusion | flops 75857920 | bytes 638976 | tf_op jit(solution)/shard_map/niab,qnic->qnabc/dot_general | solution.py:219
  192.1 2.5 copy.1142
  194.6 3.0 reshape.3290
  200.0 1.9 reshape.3308
  201.9 15.4 %all-to-all-start = ((f32[16,1,6144]{2,1,0:T(1,128)}), f32[16,1,6144]{2,1,0:T(1,128)S(1)}, u32[]{:S(2)}, u32[]{:S(2)}) async-start(f32[16,1,6144]{2,1,0:T(1,128)} %reshape.3308), calls=%async_computation | async-start | bytes 786432 | tf_op jit(solution)/shard_map/all_to_all | solution.py:170
  219.5 7.6 %all-to-all-done = f32[16,1,6144]{2,1,0:T(1,128)S(1)} async-done(((f32[16,1,6144]{2,1,0:T(1,128)}), f32[16,1,6144]{2,1,0:T(1,128)S(1)}, u32[]{:S(2)}, u32[]{:S(2)}) %all-to-all-start) | async-done | bytes 393248 | tf_op jit(solution)/shard_map/all_to_all | solution.py:170
  227.6 1.5 reduce.29
  230.9 2.6 fusion.84
  233.5 2.6 fusion.86
  236.1 2.6 fusion.113
  238.7 2.6 fusion.110
  242.5 1.9 reshape.3310
  244.4 3.6 %all-to-all-start.1 = ((f32[8,1,12288]{2,1,0:T(1,128)}), f32[8,1,12288]{2,1,0:T(1,128)S(1)}, u32[]{:S(2)}, u32[]{:S(2)}) async-start(f32[8,1,12288]{2,1,0:T(1,128)} %reshape.3310), calls=%async_computation.1 | async-start | bytes 786432 | tf_op jit(solution)/shard_map/all_to_all | solution.py:176
  249.3 6.2 %all-to-all-done.1 = f32[8,1,12288]{2,1,0:T(1,128)S(1)} async-done(((f32[8,1,12288]{2,1,0:T(1,128)}), f32[8,1,12288]{2,1,0:T(1,128)S(1)}, u32[]{:S(2)}, u32[]{:S(2)}) %all-to-all-start.1) | async-done | bytes 393248 | tf_op jit(solution)/shard_map/all_to_all | solution.py:176
  255.5 1.5 reduce.30
  258.1 1.8 copy.1285
  268.3 9.7 %all_to_all.60 = f32[8,1,12288]{2,1,0:T(1,128)S(1)} all-to-all(f32[8,1,12288]{2,1,0:T(1,128)S(1)} %reshape.3312), channel_id=1, replica_groups=mesh['row'=8,'col'=16] {'row'}, dimensions={0} | all-to-all | bytes 786432 | tf_op jit(solution)/shard_map/all_to_all | solution.py:193
  278.0 1.5 reduce.31
  280.6 1.8 copy.1284
  287.2 1.9 reshape.3314
  289.1 7.8 %all-to-all-start.3 = ((f32[16,1,6144]{2,1,0:T(1,128)}), f32[16,1,6144]{2,1,0:T(1,128)S(1)}, u32[]{:S(2)}, u32[]{:S(2)}) async-start(f32[16,1,6144]{2,1,0:T(1,128)} %reshape.3314), calls=%async_computation.3 | async-start | bytes 786432 | tf_op jit(solution)/shard_map/all_to_all | solution.py:198
  297.7 8.8 %all-to-all-done.3 = f32[16,1,6144]{2,1,0:T(1,128)S(1)} async-done(((f32[16,1,6144]{2,1,0:T(1,128)}), f32[16,1,6144]{2,1,0:T(1,128)S(1)}, u32[]{:S(2)}, u32[]{:S(2)}) %all-to-all-start.3) | async-done | bytes 393248 | tf_op jit(solution)/shard_map/all_to_all | solution.py:198
  306.5 1.5 reduce.32
  312.9 3.3 %reshape.3291 = f32[3,2,8,1,8,16,8]{6,5,4,2,1,0,3:T(8,128)} reshape(f32[3,16,8,128]{3,2,1,0:T(8,128)S(1)} %fusion.104) | data formatting | bytes 393216 | tf_op jit(solution)/shard_map/reshape | solution.py:227
  316.2 2.9 copy.1175
  319.3 4.5 %fusion.97 = f32[32,128,3]{1,2,0:T(4,128)S(1)} fusion(f32[3,32,8,8,8]{3,4,2,0,1:T(8,128)S(1)} %bitcast.577, f32[32,128,8]{1,2,0:T(8,128)S(1)} %copy-done.6, f32[32,128,8]{1,2,0:T(8,128)S(1)} %copy-done.8, f32[32,128,8]{1,2,0:T(8,128)S(1)} %copy-done.4), kind=kOutput, calls=%fused_computation.122 | convolution fusion | flops 75943936 | bytes 638976 | tf_op jit(solution)/shard_map/qnabc,niab->qnic/dot_general | solution.py:231
  (347 shorter events, 56.8 us)
Async XLA Ops:
  0.6 14.6 %copy-start.44 = (f32[3]{0:T(128)S(1)}, f32[3]{0:T(128)}, u32[]{:S(2)}) copy-start(f32[3]{0:T(128)} %constant.376.clone.1) | copy-start | bytes 40
  0.6 14.6 %copy-start.45 = (f32[3]{0:T(128)S(1)}, f32[3]{0:T(128)}, u32[]{:S(2)}) copy-start(f32[3]{0:T(128)} %constant.375.clone.1) | copy-start | bytes 40
  0.7 14.6 %copy-start.46 = (f32[3]{0:T(128)S(1)}, f32[3]{0:T(128)}, u32[]{:S(2)}) copy-start(f32[3]{0:T(128)} %constant.374.clone.1) | copy-start | bytes 40
  0.7 14.6 %copy-start.47 = (f32[3]{0:T(128)S(1)}, f32[3]{0:T(128)}, u32[]{:S(2)}) copy-start(f32[3]{0:T(128)} %constant.373.clone.1) | copy-start | bytes 40
  0.7 14.6 %copy-start.48 = (f32[3]{0:T(128)S(1)}, f32[3]{0:T(128)}, u32[]{:S(2)}) copy-start(f32[3]{0:T(128)} %constant.372.clone.1) | copy-start | bytes 40
  0.7 14.6 %copy-start.49 = (f32[3]{0:T(128)S(1)}, f32[3]{0:T(128)}, u32[]{:S(2)}) copy-start(f32[3]{0:T(128)} %constant.371.clone.1) | copy-start | bytes 40
  0.7 14.6 %copy-start = (f32[3,2,1,16,128]{4,3,2,1,0:T(8,128)S(1)}, f32[3,2,1,16,128]{4,3,2,1,0:T(8,128)}, u32[]{:S(2)}) copy-start(f32[3,2,1,16,128]{4,3,2,1,0:T(8,128)} %param.40) | copy-start | bytes 147460
  3.9 15.2 %copy-start.50 = (s32[6,2,1,16]{3,2,1,0:T(1,128)S(1)}, s32[6,2,1,16]{3,2,1,0:T(1,128)}, u32[]{:S(2)}) copy-start(s32[6,2,1,16]{3,2,1,0:T(1,128)} %param.43) | copy-start | bytes 2308
  4.7 10.7 %collective-permute-start = (f32[10,1,1,16,128]{4,3,2,1,0:T(8,128)S(1)}, f32[10,1,1,16,128]{4,3,2,1,0:T(8,128)S(1)}, u32[]{:S(2)}, u32[]{:S(2)}) collective-permute-start(f32[10,1,1,16,128]{4,3,2,1,0:T(8,128)S(1)} %get-tuple-element.221), channel_id=1, source_target_pairs={{16,0},{32,16},{48,32},{64,48},{80,64},{96,80},{112,96},{0,112},{1... | collective-permute-start | bytes 245768 | tf_op jit(solution)/shard_map/ppermute | solution.py:30
  10.3 5.4 %collective-permute-start.1 = (f32[10,1,1,16,128]{4,3,2,1,0:T(8,128)S(1)}, f32[10,1,1,16,128]{4,3,2,1,0:T(8,128)S(1)}, u32[]{:S(2)}, u32[]{:S(2)}) collective-permute-start(f32[10,1,1,16,128]{4,3,2,1,0:T(8,128)S(1)} %get-tuple-element.222), channel_id=1, source_target_pairs={{0,16},{16,32},{32,48},{48,64},{64,80},{80,96},{96,112},{112,0},{1... | collective-permute-start | bytes 245768 | tf_op jit(solution)/shard_map/ppermute | solution.py:27
  15.7 7.4 %collective-permute-start.3 = (f32[10,4,1,16,128]{4,3,2,1,0:T(8,128)S(1)}, f32[10,4,1,16,128]{4,3,2,1,0:T(8,128)S(1)}, u32[]{:S(2)}, u32[]{:S(2)}) collective-permute-start(f32[10,4,1,16,128]{4,3,2,1,0:T(8,128)S(1)} %fusion.215), channel_id=1, source_target_pairs={{0,1},{1,2},{2,3},{3,4},{4,5},{5,6},{6,7},{7,8},{8,9},{9,10},{10,1... | collective-permute-start | bytes 983048 | tf_op jit(solution)/shard_map/ppermute | solution.py:27
  19.1 6.8 %collective-permute-start.2 = (f32[10,4,1,16,128]{4,3,2,1,0:T(8,128)S(1)}, f32[10,4,1,16,128]{4,3,2,1,0:T(8,128)S(1)}, u32[]{:S(2)}, u32[]{:S(2)}) collective-permute-start(f32[10,4,1,16,128]{4,3,2,1,0:T(8,128)S(1)} %fusion.215), channel_id=1, source_target_pairs={{1,0},{2,1},{3,2},{4,3},{5,4},{6,5},{7,6},{8,7},{9,8},{10,9},{11,1... | collective-permute-start | bytes 983048 | tf_op jit(solution)/shard_map/ppermute | solution.py:30
  19.1 157.9 %copy-start.26 = (f32[1,2,1,16]{3,2,1,0:T(1,128)}, f32[1,2,1,16]{3,2,1,0:T(1,128)S(1)}, u32[]{:S(2)}) copy-start(f32[1,2,1,16]{3,2,1,0:T(1,128)S(1)} %get-tuple-element.428) | copy-start | bytes 388
  19.1 157.9 %copy-start.29 = (f32[1,2,1,16]{3,2,1,0:T(1,128)}, f32[1,2,1,16]{3,2,1,0:T(1,128)S(1)}, u32[]{:S(2)}) copy-start(f32[1,2,1,16]{3,2,1,0:T(1,128)S(1)} %get-tuple-element.429) | copy-start | bytes 388
  19.1 157.9 %copy-start.32 = (f32[1,2,1,16]{3,2,1,0:T(1,128)}, f32[1,2,1,16]{3,2,1,0:T(1,128)S(1)}, u32[]{:S(2)}) copy-start(f32[1,2,1,16]{3,2,1,0:T(1,128)S(1)} %get-tuple-element.430) | copy-start | bytes 388
  19.1 157.9 %copy-start.35 = (f32[1,2,1,16]{3,2,1,0:T(1,128)}, f32[1,2,1,16]{3,2,1,0:T(1,128)S(1)}, u32[]{:S(2)}) copy-start(f32[1,2,1,16]{3,2,1,0:T(1,128)S(1)} %get-tuple-element.431) | copy-start | bytes 388
  19.1 157.9 %copy-start.38 = (f32[1,2,1,16]{3,2,1,0:T(1,128)}, f32[1,2,1,16]{3,2,1,0:T(1,128)S(1)}, u32[]{:S(2)}) copy-start(f32[1,2,1,16]{3,2,1,0:T(1,128)S(1)} %get-tuple-element.432) | copy-start | bytes 388
  19.2 157.9 %copy-start.41 = (f32[1,2,1,16]{3,2,1,0:T(1,128)}, f32[1,2,1,16]{3,2,1,0:T(1,128)S(1)}, u32[]{:S(2)}) copy-start(f32[1,2,1,16]{3,2,1,0:T(1,128)S(1)} %get-tuple-element.433) | copy-start | bytes 388
  59.5 3.8 %copy-start.1 = (f32[3,2,1,16,128]{4,3,2,1,0:T(8,128)S(1)}, f32[3,2,1,16,128]{4,3,2,1,0:T(8,128)}, u32[]{:S(2)}) copy-start(f32[3,2,1,16,128]{4,3,2,1,0:T(8,128)} %param.41) | copy-start | bytes 147460
  63.8 4.0 %collective-permute-start.4 = (f32[10,1,1,16,128]{4,3,2,1,0:T(8,128)S(1)}, f32[10,1,1,16,128]{4,3,2,1,0:T(8,128)S(1)}, u32[]{:S(2)}, u32[]{:S(2)}) collective-permute-start(f32[10,1,1,16,128]{4,3,2,1,0:T(8,128)S(1)} %get-tuple-element.217), channel_id=1, source_target_pairs={{16,0},{32,16},{48,32},{64,48},{80,64},{96,80},{112,96},{0,112},{1... | collective-permute-start | bytes 245768 | tf_op jit(solution)/shard_map/ppermute | solution.py:30
  66.3 5.4 %collective-permute-start.5 = (f32[10,1,1,16,128]{4,3,2,1,0:T(8,128)S(1)}, f32[10,1,1,16,128]{4,3,2,1,0:T(8,128)S(1)}, u32[]{:S(2)}, u32[]{:S(2)}) collective-permute-start(f32[10,1,1,16,128]{4,3,2,1,0:T(8,128)S(1)} %get-tuple-element.218), channel_id=1, source_target_pairs={{0,16},{16,32},{32,48},{48,64},{64,80},{80,96},{96,112},{112,0},{1... | collective-permute-start | bytes 245768 | tf_op jit(solution)/shard_map/ppermute | solution.py:27
  71.7 5.7 %collective-permute-start.7 = (f32[10,4,1,16,128]{4,3,2,1,0:T(8,128)S(1)}, f32[10,4,1,16,128]{4,3,2,1,0:T(8,128)S(1)}, u32[]{:S(2)}, u32[]{:S(2)}) collective-permute-start(f32[10,4,1,16,128]{4,3,2,1,0:T(8,128)S(1)} %fusion.217), channel_id=1, source_target_pairs={{0,1},{1,2},{2,3},{3,4},{4,5},{5,6},{6,7},{7,8},{8,9},{9,10},{10,1... | collective-permute-start | bytes 983048 | tf_op jit(solution)/shard_map/ppermute | solution.py:27
  73.4 6.5 %collective-permute-start.6 = (f32[10,4,1,16,128]{4,3,2,1,0:T(8,128)S(1)}, f32[10,4,1,16,128]{4,3,2,1,0:T(8,128)S(1)}, u32[]{:S(2)}, u32[]{:S(2)}) collective-permute-start(f32[10,4,1,16,128]{4,3,2,1,0:T(8,128)S(1)} %fusion.217), channel_id=1, source_target_pairs={{1,0},{2,1},{3,2},{4,3},{5,4},{6,5},{7,6},{8,7},{9,8},{10,9},{11,1... | collective-permute-start | bytes 983048 | tf_op jit(solution)/shard_map/ppermute | solution.py:30
  117.5 3.4 %collective-permute-start.8 = (f32[10,1,1,16,128]{4,3,2,1,0:T(8,128)S(1)}, f32[10,1,1,16,128]{4,3,2,1,0:T(8,128)S(1)}, u32[]{:S(2)}, u32[]{:S(2)}) collective-permute-start(f32[10,1,1,16,128]{4,3,2,1,0:T(8,128)S(1)} %get-tuple-element.213), channel_id=1, source_target_pairs={{16,0},{32,16},{48,32},{64,48},{80,64},{96,80},{112,96},{0,112},{1... | collective-permute-start | bytes 245768 | tf_op jit(solution)/shard_map/ppermute | solution.py:30
  117.6 5.5 %collective-permute-start.9 = (f32[10,1,1,16,128]{4,3,2,1,0:T(8,128)S(1)}, f32[10,1,1,16,128]{4,3,2,1,0:T(8,128)S(1)}, u32[]{:S(2)}, u32[]{:S(2)}) collective-permute-start(f32[10,1,1,16,128]{4,3,2,1,0:T(8,128)S(1)} %get-tuple-element.214), channel_id=1, source_target_pairs={{0,16},{16,32},{32,48},{48,64},{64,80},{80,96},{96,112},{112,0},{1... | collective-permute-start | bytes 245768 | tf_op jit(solution)/shard_map/ppermute | solution.py:27
  123.1 8.0 %collective-permute-start.11 = (f32[10,4,1,16,128]{4,3,2,1,0:T(8,128)S(1)}, f32[10,4,1,16,128]{4,3,2,1,0:T(8,128)S(1)}, u32[]{:S(2)}, u32[]{:S(2)}) collective-permute-start(f32[10,4,1,16,128]{4,3,2,1,0:T(8,128)S(1)} %fusion.219), channel_id=1, source_target_pairs={{0,1},{1,2},{2,3},{3,4},{4,5},{5,6},{6,7},{7,8},{8,9},{9,10},{10,1... | collective-permute-start | bytes 983048 | tf_op jit(solution)/shard_map/ppermute | solution.py:27
  124.4 6.9 %collective-permute-start.10 = (f32[10,4,1,16,128]{4,3,2,1,0:T(8,128)S(1)}, f32[10,4,1,16,128]{4,3,2,1,0:T(8,128)S(1)}, u32[]{:S(2)}, u32[]{:S(2)}) collective-permute-start(f32[10,4,1,16,128]{4,3,2,1,0:T(8,128)S(1)} %fusion.219), channel_id=1, source_target_pairs={{1,0},{2,1},{3,2},{4,3},{5,4},{6,5},{7,6},{8,7},{9,8},{10,9},{11,1... | collective-permute-start | bytes 983048 | tf_op jit(solution)/shard_map/ppermute | solution.py:30
  177.3 14.7 %copy-start.3 = (f32[32,128,8]{1,2,0:T(8,128)}, f32[32,128,8]{1,2,0:T(8,128)S(1)}, u32[]{:S(2)}) copy-start(f32[32,128,8]{1,2,0:T(8,128)S(1)} %get-tuple-element.434) | copy-start | bytes 393220
  177.4 14.7 %copy-start.5 = (f32[32,128,8]{1,2,0:T(8,128)}, f32[32,128,8]{1,2,0:T(8,128)S(1)}, u32[]{:S(2)}) copy-start(f32[32,128,8]{1,2,0:T(8,128)S(1)} %get-tuple-element.435) | copy-start | bytes 393220
  177.4 14.7 %copy-start.7 = (f32[32,128,8]{1,2,0:T(8,128)}, f32[32,128,8]{1,2,0:T(8,128)S(1)}, u32[]{:S(2)}) copy-start(f32[32,128,8]{1,2,0:T(8,128)S(1)} %get-tuple-element.436) | copy-start | bytes 393220
  201.9 25.2 %all-to-all-start = ((f32[16,1,6144]{2,1,0:T(1,128)}), f32[16,1,6144]{2,1,0:T(1,128)S(1)}, u32[]{:S(2)}, u32[]{:S(2)}) async-start(f32[16,1,6144]{2,1,0:T(1,128)} %reshape.3308), calls=%async_computation | async-start | bytes 786432 | tf_op jit(solution)/shard_map/all_to_all | solution.py:170
  242.5 6.1 %copy-start.54 = (f32[16]{0:T(128)S(1)}, f32[16]{0:T(128)}, u32[]{:S(2)}) copy-start(f32[16]{0:T(128)} %fusion.482) | copy-start | bytes 196
  244.4 11.1 %all-to-all-start.1 = ((f32[8,1,12288]{2,1,0:T(1,128)}), f32[8,1,12288]{2,1,0:T(1,128)S(1)}, u32[]{:S(2)}, u32[]{:S(2)}) async-start(f32[8,1,12288]{2,1,0:T(1,128)} %reshape.3310), calls=%async_computation.1 | async-start | bytes 786432 | tf_op jit(solution)/shard_map/all_to_all | solution.py:176
  287.0 9.8 %copy-start.19 = (f32[1,32,128]{2,0,1:T(1,128)S(1)}, f32[1,32,128]{2,0,1:T(1,128)}, u32[]{:S(2)}) copy-start(f32[1,32,128]{2,0,1:T(1,128)} %get-tuple-element.227) | copy-start | bytes 49156
  287.0 9.8 %copy-start.20 = (f32[1,32,128]{2,0,1:T(1,128)S(1)}, f32[1,32,128]{2,0,1:T(1,128)}, u32[]{:S(2)}) copy-start(f32[1,32,128]{2,0,1:T(1,128)} %get-tuple-element.231) | copy-start | bytes 49156
  287.0 9.8 %copy-start.21 = (f32[1,32,128]{2,0,1:T(1,128)S(1)}, f32[1,32,128]{2,0,1:T(1,128)}, u32[]{:S(2)}) copy-start(f32[1,32,128]{2,0,1:T(1,128)} %get-tuple-element.247) | copy-start | bytes 49156
  287.1 9.8 %copy-start.22 = (f32[1,32,128]{2,0,1:T(1,128)S(1)}, f32[1,32,128]{2,0,1:T(1,128)}, u32[]{:S(2)}) copy-start(f32[1,32,128]{2,0,1:T(1,128)} %get-tuple-element.235) | copy-start | bytes 49156
  287.1 9.8 %copy-start.23 = (f32[1,32,128]{2,0,1:T(1,128)S(1)}, f32[1,32,128]{2,0,1:T(1,128)}, u32[]{:S(2)}) copy-start(f32[1,32,128]{2,0,1:T(1,128)} %get-tuple-element.239) | copy-start | bytes 49156
  287.1 9.8 %copy-start.24 = (f32[1,32,128]{2,0,1:T(1,128)S(1)}, f32[1,32,128]{2,0,1:T(1,128)}, u32[]{:S(2)}) copy-start(f32[1,32,128]{2,0,1:T(1,128)} %get-tuple-element.243) | copy-start | bytes 49156
  287.1 9.8 %copy-start.25 = (f32[1,32,128]{2,0,1:T(1,128)S(1)}, f32[1,32,128]{2,0,1:T(1,128)}, u32[]{:S(2)}) copy-start(f32[1,32,128]{2,0,1:T(1,128)} %get-tuple-element.223) | copy-start | bytes 49156
  287.1 9.8 %copy-start.27 = (f32[1,2,1,16]{3,2,1,0:T(1,128)S(1)}, f32[1,2,1,16]{3,2,1,0:T(1,128)}, u32[]{:S(2)}) copy-start(f32[1,2,1,16]{3,2,1,0:T(1,128)} %copy-done.26) | copy-start | bytes 388
  287.1 9.8 %copy-start.30 = (f32[1,2,1,16]{3,2,1,0:T(1,128)S(1)}, f32[1,2,1,16]{3,2,1,0:T(1,128)}, u32[]{:S(2)}) copy-start(f32[1,2,1,16]{3,2,1,0:T(1,128)} %copy-done.29) | copy-start | bytes 388
  287.1 9.8 %copy-start.33 = (f32[1,2,1,16]{3,2,1,0:T(1,128)S(1)}, f32[1,2,1,16]{3,2,1,0:T(1,128)}, u32[]{:S(2)}) copy-start(f32[1,2,1,16]{3,2,1,0:T(1,128)} %copy-done.32) | copy-start | bytes 388
  287.1 9.8 %copy-start.36 = (f32[1,2,1,16]{3,2,1,0:T(1,128)S(1)}, f32[1,2,1,16]{3,2,1,0:T(1,128)}, u32[]{:S(2)}) copy-start(f32[1,2,1,16]{3,2,1,0:T(1,128)} %copy-done.35) | copy-start | bytes 388
  287.1 9.8 %copy-start.39 = (f32[1,2,1,16]{3,2,1,0:T(1,128)S(1)}, f32[1,2,1,16]{3,2,1,0:T(1,128)}, u32[]{:S(2)}) copy-start(f32[1,2,1,16]{3,2,1,0:T(1,128)} %copy-done.38) | copy-start | bytes 388
  287.1 9.8 %copy-start.42 = (f32[1,2,1,16]{3,2,1,0:T(1,128)S(1)}, f32[1,2,1,16]{3,2,1,0:T(1,128)}, u32[]{:S(2)}) copy-start(f32[1,2,1,16]{3,2,1,0:T(1,128)} %copy-done.41) | copy-start | bytes 388
  289.1 17.5 %all-to-all-start.3 = ((f32[16,1,6144]{2,1,0:T(1,128)}), f32[16,1,6144]{2,1,0:T(1,128)S(1)}, u32[]{:S(2)}, u32[]{:S(2)}) async-start(f32[16,1,6144]{2,1,0:T(1,128)} %reshape.3314), calls=%async_computation.3 | async-start | bytes 786432 | tf_op jit(solution)/shard_map/all_to_all | solution.py:198
  316.2 3.1 copy-start.6
  316.2 3.1 copy-start.8
  319.1 4.7 %copy-start.2 = (f32[3,2,1,16,128]{4,3,2,1,0:T(8,128)S(1)}, f32[3,2,1,16,128]{4,3,2,1,0:T(8,128)}, u32[]{:S(2)}) copy-start(f32[3,2,1,16,128]{4,3,2,1,0:T(8,128)} %param.41) | copy-start | bytes 147460
  319.1 4.7 %copy-start.9 = (f32[3,32,128]{2,0,1:T(4,128)S(1)}, f32[3,32,128]{2,0,1:T(4,128)}, u32[]{:S(2)}) copy-start(f32[3,32,128]{2,0,1:T(4,128)} %get-tuple-element.253) | copy-start | bytes 147460
  319.1 4.7 %copy-start.10 = (f32[3,32,128]{2,0,1:T(4,128)S(1)}, f32[3,32,128]{2,0,1:T(4,128)}, u32[]{:S(2)}) copy-start(f32[3,32,128]{2,0,1:T(4,128)} %get-tuple-element.255) | copy-start | bytes 147460
  319.2 4.7 %copy-start.11 = (f32[3,32,128]{2,0,1:T(4,128)S(1)}, f32[3,32,128]{2,0,1:T(4,128)}, u32[]{:S(2)}) copy-start(f32[3,32,128]{2,0,1:T(4,128)} %get-tuple-element.263) | copy-start | bytes 147460
  319.2 4.7 %copy-start.12 = (f32[3,32,128]{2,0,1:T(4,128)S(1)}, f32[3,32,128]{2,0,1:T(4,128)}, u32[]{:S(2)}) copy-start(f32[3,32,128]{2,0,1:T(4,128)} %get-tuple-element.257) | copy-start | bytes 147460
  319.2 4.7 %copy-start.13 = (f32[3,32,128]{2,0,1:T(4,128)S(1)}, f32[3,32,128]{2,0,1:T(4,128)}, u32[]{:S(2)}) copy-start(f32[3,32,128]{2,0,1:T(4,128)} %get-tuple-element.259) | copy-start | bytes 147460
  319.2 4.7 %copy-start.14 = (f32[3,32,128]{2,0,1:T(4,128)S(1)}, f32[3,32,128]{2,0,1:T(4,128)}, u32[]{:S(2)}) copy-start(f32[3,32,128]{2,0,1:T(4,128)} %get-tuple-element.261) | copy-start | bytes 147460
  319.2 4.7 %copy-start.15 = (f32[3,32,128]{2,0,1:T(4,128)S(1)}, f32[3,32,128]{2,0,1:T(4,128)}, u32[]{:S(2)}) copy-start(f32[3,32,128]{2,0,1:T(4,128)} %get-tuple-element.251) | copy-start | bytes 147460
  319.2 4.7 %copy-start.18 = (f32[2,16,128]{2,1,0:T(8,128)S(1)}, f32[2,16,128]{2,1,0:T(8,128)}, u32[]{:S(2)}) copy-start(f32[2,16,128]{2,1,0:T(8,128)} %multiply_add_fusion) | copy-start | bytes 49156
  319.2 4.7 %copy-start.28 = (f32[1,2,1,16]{3,2,1,0:T(1,128)S(1)}, f32[1,2,1,16]{3,2,1,0:T(1,128)}, u32[]{:S(2)}) copy-start(f32[1,2,1,16]{3,2,1,0:T(1,128)} %copy-done.26) | copy-start | bytes 388
  319.2 4.7 %copy-start.31 = (f32[1,2,1,16]{3,2,1,0:T(1,128)S(1)}, f32[1,2,1,16]{3,2,1,0:T(1,128)}, u32[]{:S(2)}) copy-start(f32[1,2,1,16]{3,2,1,0:T(1,128)} %copy-done.29) | copy-start | bytes 388
  319.2 4.7 %copy-start.34 = (f32[1,2,1,16]{3,2,1,0:T(1,128)S(1)}, f32[1,2,1,16]{3,2,1,0:T(1,128)}, u32[]{:S(2)}) copy-start(f32[1,2,1,16]{3,2,1,0:T(1,128)} %copy-done.32) | copy-start | bytes 388
  319.3 4.7 %copy-start.37 = (f32[1,2,1,16]{3,2,1,0:T(1,128)S(1)}, f32[1,2,1,16]{3,2,1,0:T(1,128)}, u32[]{:S(2)}) copy-start(f32[1,2,1,16]{3,2,1,0:T(1,128)} %copy-done.35) | copy-start | bytes 388
  319.3 4.7 %copy-start.40 = (f32[1,2,1,16]{3,2,1,0:T(1,128)S(1)}, f32[1,2,1,16]{3,2,1,0:T(1,128)}, u32[]{:S(2)}) copy-start(f32[1,2,1,16]{3,2,1,0:T(1,128)} %copy-done.38) | copy-start | bytes 388
  319.3 4.7 %copy-start.43 = (f32[1,2,1,16]{3,2,1,0:T(1,128)S(1)}, f32[1,2,1,16]{3,2,1,0:T(1,128)}, u32[]{:S(2)}) copy-start(f32[1,2,1,16]{3,2,1,0:T(1,128)} %copy-done.41) | copy-start | bytes 388
  (7 other events, 17.5 us)
where the time goes:
time: 330 us; the launch traced here: 325 us
  matrix products  110 us (33%)
  other arithmetic  56.5 us (17%)
  local copies, waits for them, and re-layouts  51.7 us (16%)
  starting transfers between devices  50.5 us (15%)
  waiting for transfers between devices  43.7 us (13%)
  blocking collectives  9.69 us (3%)
  between operations  3.38 us (1%)
    dot_general x21, matrix products, pair_totals(): return jnp.einsum('nij,qnj->qni', weights, far_loads, precision=highest)  71.5 us
    reduce_sum x3, other arithmetic, pair_totals(): jnp.sum(separation * separation, axis=0)  37.2 us
    ppermute x6, starting transfers between devices, with_halo(): lax.ppermute(lax.slice_in_dim(block, 0, width, axis=dim), axis, backward)  15.9 us
    all_to_all x1, starting transfers between devices, solve_far(): lax.all_to_all(spectrum, 'col', split_axis=2, concat_axis=4, tiled=True)  15.4 us
    dot_general x1, matrix products, far_field(): cubes = jnp.einsum('niab,qnic->qnabc', planar, lifted, precision=highest)  14.3 us
    ppermute x6, waiting for transfers between devices, with_halo(): lax.ppermute(lax.slice_in_dim(block, block.shape[dim] - width, None, axis...  12.4 us
    unnamed x121, local copies, waits for them, and re-layouts  12.2 us
    all_to_all x1, blocking collectives, solve_far(): lax.all_to_all(pencil, 'row', split_axis=4, concat_axis=2, tiled=True)  9.69 us
  transfers between devices with their start and end apart: 15, of which 14 were waited for; matrix products, arithmetic and copies ran while one was open for 3% of the time, Pallas kernels for 0%

commit v1 on v0

v1 whole, which is shorter than its diff:
```python
import math

import jax
import jax.numpy as jnp
import numpy as np
from jax import lax
from jax.experimental import pallas as pl
from jax.experimental.pallas import tpu as pltpu
from jax.sharding import PartitionSpec as P

GRID = 128
CELL = 8
SLOT = 128
STEPS = 3
ROWS = 8
COLS = 16
DEVICES = ROWS * COLS
CELLS = 32
HALF = 16
MESH = pl.DeviceIdType.MESH
F32 = jnp.float32
BF16 = jnp.bfloat16

KAPPA = 2.0 / (CELL * CELL) * math.log2(math.e)
PACE = 0.06 * CELL
DRIFT = 1.0 / SLOT
COUPLE = 0.5 / SLOT
MID = 0.5 * CELL

A_ROWS = 48
B_ROWS = 16
L_ROWS = 16


def narrow(v):
    return v.astype(BF16).astype(F32)


def split3(v):
    h = narrow(v)
    r = v - h
    m = narrow(r)
    return h, m, r - m


def put(ref, lead, start, stride, val):
    ref[lead, pl.ds(start, val.shape[0], stride=stride), :] = val


def put_receiver(afeat, half, px, py, pz):
    base = half * HALF * A_ROWS

    def row(k, v):
        afeat[pl.ds(base + k, HALF, stride=A_ROWS), :] = v

    parts = [split3(v * (2.0 * KAPPA)) for v in (px, py, pz)]
    size = split3(-KAPPA * (px * px + py * py + pz * pz))
    for d in range(3):
        h, m, l = parts[d]
        row(d, h)
        row(8 + d, h)
        row(11 + d, h)
        row(16 + d, m)
        row(24 + d, m)
        row(32 + d, l)
    row(6, size[0])
    row(16 + 6, size[1])
    row(32 + 6, size[2])


def put_source(bfeat, lfeat, slot, half, place, torque, fill, shift, gate):
    place = [place[d] + shift[d] if shift[d] != 0.0 else place[d] for d in range(3)]
    x, y, z = place
    base = half * HALF * B_ROWS
    for d in range(3):
        h, m, l = split3(place[d])
        put(bfeat, slot, base + d, B_ROWS, h)
        put(bfeat, slot, base + 8 + d, B_ROWS, m)
        put(bfeat, slot, base + 11 + d, B_ROWS, l)
    for k, v in enumerate(split3(-KAPPA * (x * x + y * y + z * z))):
        put(bfeat, slot, base + 3 + k, B_ROWS, v)
    if gate is not None:
        torque = [t * gate for t in torque]
        fill = fill * gate
    tx, ty, tz = torque
    loads = (tx, ty, tz, ty * z - tz * y, tz * x - tx * z, tx * y - ty * x)
    base = half * HALF * L_ROWS
    for q, v in enumerate(loads):
        h = narrow(v)
        put(lfeat, slot, base + q, L_ROWS, h)
        put(lfeat, slot, base + 8 + q, L_ROWS, v - h)
    put(lfeat, slot, base + 6, L_ROWS, fill)


def near_kernel(
    pos_in, tor_in, cnt, flg, pos_out, near_out, fill_out,
    state, places, gates, afeat, trans, bfeat, lfeat, totals,
    full_x, full_y, part_x, part_y, send_sem, recv_sem,
):
    row = lax.axis_index("row")
    col = lax.axis_index("col")
    peers = (
        (lax.rem(row + 1, ROWS), col),
        (lax.rem(row + ROWS - 1, ROWS), col),
        (row, lax.rem(col + 1, COLS)),
        (row, lax.rem(col + COLS - 1, COLS)),
    )
    barrier = pltpu.get_barrier_semaphore()
    for peer in peers:
        pl.semaphore_signal(barrier, inc=1, device_id=peer, device_id_type=MESH)

    lane = lax.broadcasted_iota(jnp.int32, (1, SLOT), 1)

    def spread_scalars(z, carry):
        for h in range(2):
            state[6, pl.ds(h * HALF + z, 1), :] = (lane < cnt[h, 0, z]).astype(F32)
            for f in range(6):
                gates[f, pl.ds(h * HALF + z, 1), :] = jnp.full((1, SLOT), flg[f, h, 0, z], jnp.int32).astype(F32)
        return carry

    lax.fori_loop(0, HALF, spread_scalars, 0)
    fill = state[6]
    fill_out[...] = fill
    for d in range(3):
        state[d] = pos_in[d] - MID
        state[3 + d] = tor_in[d] * fill

    pl.semaphore_wait(barrier, 4)

    def halo(step):
        if step == 0:
            own, into_x, into_y = state, full_x, full_y
        else:
            own, into_x, into_y = places.at[step - 1], part_x.at[step - 1], part_y.at[step - 1]
        moves = (
            (own.at[:, pl.ds(HALF, HALF), :], into_x.at[0], 0),
            (own.at[:, pl.ds(0, HALF), :], into_x.at[1], 1),
            (own, into_y.at[0], 2),
            (own, into_y.at[1], 3),
        )
        copies = []
        for src, dst, k in moves:
            copies.append(
                pltpu.make_async_remote_copy(
                    src_ref=src,
                    dst_ref=dst,
                    send_sem=send_sem.at[step, k],
                    recv_sem=recv_sem.at[step, k],
                    device_id=peers[k],
                    device_id_type=MESH,
                )
            )
        return copies

    one = jnp.ones((CELLS, SLOT), F32)
    zero = jnp.zeros((CELLS, SLOT), F32)
    for k in (7, 14, 15, 19, 20, 21, 23, 27, 28, 29, 30, 31, 35, 36, 37, 39, *range(40, 48)):
        afeat[pl.ds(k, CELLS, stride=A_ROWS), :] = zero
    for k in (3, 4, 5):
        afeat[pl.ds(k, CELLS, stride=A_ROWS), :] = one
    for e in range(7):
        put(bfeat, e, 6, B_ROWS, one)
        for k in (7, 14, 15):
            put(bfeat, e, k, B_ROWS, zero)
        for k in (7, 14, 15):
            put(lfeat, e, k, L_ROWS, zero)

    def weighted(at, cell, faces):
        def wide(ref, n):
            blocks = [ref[e, pl.ds(pl.multiple_of(cell * n, n), n), :] for e in faces]
            return (blocks[0] if len(blocks) == 1 else jnp.concatenate(blocks, 1)).astype(BF16)

        b = wide(bfeat, B_ROWS)
        b = jnp.concatenate([b, b, b], 0)
        power = jnp.dot(at, b, preferred_element_type=F32)
        w = jnp.exp2(power).astype(BF16)
        return lax.dot_general(wide(lfeat, L_ROWS), w, (((1,), (1,)), ((), ())), preferred_element_type=F32)

    def inner_faces(z, carry):
        for h in range(2):
            cell = h * HALF + z
            at = afeat[pl.ds(pl.multiple_of(cell * A_ROWS, A_ROWS), A_ROWS), :].T.astype(BF16)
            trans[cell] = at
            acc = weighted(at, cell, (0, 1)) + weighted(at, cell, (2, 3))
            totals[pl.ds(pl.multiple_of(cell * 8, 8), 8), :] = acc[0:8] + acc[8:16]
        return carry

    def outer_faces(z, carry):
        for h in range(2):
            cell = h * HALF + z
            at = trans[cell]
            acc = weighted(at, cell, (4, 5)) + weighted(at, cell, (6,))
            spot = pl.ds(pl.multiple_of(cell * 8, 8), 8)
            totals[spot, :] = totals[spot, :] + (acc[0:8] + acc[8:16])
        return carry

    for step in range(STEPS):
        copies = halo(step)
        for copy in copies:
            copy.start()
        here = state if step == 0 else places.at[step - 1]
        for h in range(2):
            part = slice(h * HALF, (h + 1) * HALF)
            other = slice((1 - h) * HALF, (2 - h) * HALF)
            place = [here[d, part, :] for d in range(3)]
            torque = [state[3 + d, part, :] for d in range(3)]
            fill = state[6, part, :]
            put_receiver(afeat, h, *place)
            put_source(bfeat, lfeat, 0, h, place, torque, fill, (0.0, 0.0, 0.0), None)
            for slot, turn, lift, face in ((1, HALF - 1, CELL, 4), (2, 1, -CELL, 5)):
                def turned(v):
                    return pltpu.roll(v, turn, 0)

                put_source(
                    bfeat, lfeat, slot, h, [turned(v) for v in place], [turned(v) for v in torque], turned(fill),
                    (0.0, 0.0, float(lift)), gates[face, part, :],
                )
            put_source(
                bfeat, lfeat, 3, h,
                [here[d, other, :] for d in range(3)],
                [state[3 + d, other, :] for d in range(3)],
                state[6, other, :],
                (float(CELL) if h == 0 else -float(CELL), 0.0, 0.0),
                gates[0 if h == 0 else 1, part, :],
            )
        lax.fori_loop(0, HALF, inner_faces, 0)
        for copy in copies:
            copy.wait_recv()
        for h in range(2):
            part = slice(h * HALF, (h + 1) * HALF)
            near_x = full_x if step == 0 else part_x.at[step - 1]
            near_y = full_y if step == 0 else part_y.at[step - 1]
            put_source(
                bfeat, lfeat, 4, h,
                [near_x[h, d] for d in range(3)],
                [full_x[h, 3 + d] for d in range(3)],
                full_x[h, 6],
                (-float(CELL) if h == 0 else float(CELL), 0.0, 0.0),
                gates[1 if h == 0 else 0, part, :],
            )
            for slot, side, lift, face in ((5, 1, CELL, 2), (6, 0, -CELL, 3)):
                put_source(
                    bfeat, lfeat, slot, h,
                    [near_y[side, d, part, :] for d in range(3)],
                    [full_y[side, 3 + d, part, :] for d in range(3)],
                    full_y[side, 6, part, :],
                    (0.0, float(lift), 0.0),
                    gates[face, part, :],
                )
        lax.fori_loop(0, HALF, outer_faces, 0)

        tot = [totals[pl.ds(q, CELLS, stride=8), :] for q in range(7)]
        fill = state[6]
        x, y, z = (here[d] for d in range(3))
        speed = (
            tot[1] * z - tot[2] * y - tot[3],
            tot[2] * x - tot[0] * z - tot[4],
            tot[0] * y - tot[1] * x - tot[5],
        )
        for d in range(3):
            moved = here[d] + PACE * (DRIFT * speed[d] * fill)
            if step < STEPS - 1:
                places[step, d] = moved
            else:
                pos_out[d] = moved + MID
                torque = tor_in[d]
                near_out[d] = (torque + COUPLE * (tot[d] - tot[6] * torque)) * fill

    for step in range(STEPS):
        for copy in halo(step):
            copy.wait_send()


def near_field(positions, torques, counts, flags):
    vmem = pl.BlockSpec(memory_space=pltpu.VMEM)
    smem = pl.BlockSpec(memory_space=pltpu.SMEM)
    field = jax.ShapeDtypeStruct((3, CELLS, SLOT), F32)
    return pl.pallas_call(
        near_kernel,
        name="near",
        out_shape=(field, field, jax.ShapeDtypeStruct((CELLS, SLOT), F32)),
        in_specs=[vmem, vmem, smem, smem],
        out_specs=(vmem, vmem, vmem),
        scratch_shapes=[
            pltpu.VMEM((7, CELLS, SLOT), F32),
            pltpu.VMEM((STEPS - 1, 3, CELLS, SLOT), F32),
            pltpu.VMEM((6, CELLS, SLOT), F32),
            pltpu.VMEM((CELLS * A_ROWS, SLOT), F32),
            pltpu.VMEM((CELLS, SLOT, A_ROWS), BF16),
            pltpu.VMEM((7, CELLS * B_ROWS, SLOT), F32),
            pltpu.VMEM((7, CELLS * L_ROWS, SLOT), F32),
            pltpu.VMEM((CELLS * 8, SLOT), F32),
            pltpu.VMEM((2, 7, HALF, SLOT), F32),
            pltpu.VMEM((2, 7, CELLS, SLOT), F32),
            pltpu.VMEM((STEPS - 1, 2, 3, HALF, SLOT), F32),
            pltpu.VMEM((STEPS - 1, 2, 3, CELLS, SLOT), F32),
            pltpu.SemaphoreType.DMA((STEPS, 4)),
            pltpu.SemaphoreType.DMA((STEPS, 4)),
        ],
        compiler_params=pltpu.CompilerParams(collective_id=0, has_side_effects=True),
    )(positions, torques, counts, flags)


def halves(table):
    high = table.astype(np.float32).astype(jnp.bfloat16)
    low = (table - high.astype(np.float64)).astype(np.float32).astype(jnp.bfloat16)
    return high, low


def make_tables():
    n = np.arange(GRID)
    level = np.where(n == 1, 64, n // 2)
    angle = 2.0 * np.pi * (level[:, None] * n[None, :] % GRID) / GRID
    cosine, sine = np.cos(angle), np.sin(angle)
    even = (n % 2 == 0)[:, None]
    whole = (n < 2)[:, None]
    basis_xy = np.where(whole | even, cosine, sine)
    basis_z = np.where(whole | ~even, cosine, sine)
    count = np.where(n < 2, 1.0, 2.0)[:, None]
    back_xy, back_z = (basis_xy * count).T, (basis_z * count).T

    def wave(a, b, period_a, period_b):
        return 2.0 * np.pi * ((a * b[0] % period_a) / period_a + (b[1] % period_b) / period_b)

    r, q = n // 16, n % 16
    turn_l = 2.0 * np.pi * ((r[:, None] * r[None, :] % 8) / 8 + (q[:, None] * q[None, :] % 16) / 16)
    s, t = n // 8, n % 8
    turn_r = 2.0 * np.pi * ((s[:, None] * s[None, :] % 16) / 16 + (t[:, None] * t[None, :] % 8) / 8)
    twist = 2.0 * np.pi * (r[:, None] * s[None, :] + q[:, None] * t[None, :]) / GRID
    cl, sl = np.cos(turn_l), np.sin(turn_l)
    cr, sr = np.cos(turn_r), np.sin(turn_r)
    left = np.concatenate([cl, -sl], 0)
    left_back = np.concatenate([cl, -sl], 1)
    right = np.block([[cr, -sr], [sr, cr]])
    right_back = np.block([[cr, sr], [-sr, cr]])
    out = []
    for table in (basis_xy, basis_z, back_xy, back_z, left, left_back, right, right_back):
        high, low = halves(table)
        out += [high, low]
    out.append(np.stack([np.cos(twist), np.sin(twist)]).astype(np.float32))
    return out


def cut(v):
    h = v.astype(BF16)
    return h, (v - h.astype(F32)).astype(BF16)


def mul(a, b):
    return jnp.dot(a, b, preferred_element_type=F32)


def mul_t(a, b):
    return lax.dot_general(a, b, (((1,), (1,)), ((), ())), preferred_element_type=F32)


def table_left(high, low, v):
    vh, vl = cut(v)
    return mul(high, vh) + (mul(low, vh) + mul(high, vl))


def table_right(v, high, low):
    vh, vl = cut(v)
    return mul(vh, high) + (mul(vl, high) + mul(vh, low))


def far_kernel(
    pos, tor, near, fill, zf_xy_h, zf_xy_l, zf_z_h, zf_z_l, zb_xy_h, zb_xy_l, zb_z_h, zb_z_l,
    lf_h, lf_l, lb_h, lb_l, rf_h, rf_l, rb_h, rb_l, twist,
    spin,
    grid, plan_h, plan_l, depth, out_1, in_1, out_2, in_2, work, far, send_sem, recv_sem, self_sem,
):
    row = lax.axis_index("row")
    col = lax.axis_index("col")
    me = row * COLS + col
    barrier = pltpu.get_barrier_semaphore()

    def peer(k):
        p = lax.rem(me + k, DEVICES)
        return p, (p // COLS, lax.rem(p, COLS))

    def greet(k, carry):
        pl.semaphore_signal(barrier, inc=1, device_id=peer(k)[1], device_id_type=MESH)
        return carry

    lax.fori_loop(1, DEVICES, greet, 0)

    level = lax.broadcasted_iota(jnp.int32, (CELL, SLOT), 0).astype(F32) + 0.5
    low_lane = lax.broadcasted_iota(jnp.int32, (24, SLOT), 1) < 64

    def bins(d, cell):
        apart = pos[d, pl.ds(cell, 1), :] - level
        return jnp.exp(-apart * apart)

    def spread(z, carry):
        planar, lifted, rest = [], [], []
        for h in range(2):
            cell = h * HALF + z
            bx, by, bz = (bins(d, cell) for d in range(3))
            depth[pl.ds(pl.multiple_of(cell * 8, 8), 8), :] = bz
            planar += [bx[a : a + 1, :] * by for a in range(CELL)]
            lift = [tor[c, pl.ds(cell, 1), :] * fill[pl.ds(cell, 1), :] * bz for c in range(3)]
            top = [narrow(v) for v in lift]
            lifted += top
            rest += [v - t for v, t in zip(lift, top)]
        ph, pl_ = cut(jnp.concatenate(planar, 0))
        plan_h[z] = ph
        plan_l[z] = pl_
        both = mul_t(jnp.concatenate(lifted + rest, 0).astype(BF16), ph)
        more = mul_t(jnp.concatenate(lifted, 0).astype(BF16), pl_)
        sums = both[0:48] + both[48:96] + more
        block = jnp.where(low_lane, sums[0:24], sums[24:48])
        for c in range(3):
            grid[c, pl.ds(pl.multiple_of(z * 8, 8), 8), :] = block[c * 8 : c * 8 + 8]
        return carry

    lax.fori_loop(0, HALF, spread, 0)

    for c in range(3):
        high, low = (zf_xy_h, zf_xy_l) if c < 2 else (zf_z_h, zf_z_l)
        out_1[pl.ds(c, DEVICES, stride=8), :] = table_left(high[...], low[...], grid[c])

    pl.semaphore_wait(barrier, DEVICES - 1)

    def exchange(out, into, k):
        def post(i, carry):
            p, where = peer(i)
            pltpu.make_async_remote_copy(
                src_ref=out.at[pl.ds(pl.multiple_of(p * 8, 8), 3), :],
                dst_ref=into.at[pl.ds(pl.multiple_of(me * 8, 8), 3), :],
                send_sem=send_sem.at[k],
                recv_sem=recv_sem.at[k],
                device_id=where,
                device_id_type=MESH,
            ).start()
            return carry

        lax.fori_loop(1, DEVICES, post, 0)
        mine = pl.ds(pl.multiple_of(me * 8, 8), 3)
        keep = pltpu.make_async_copy(out.at[mine, :], into.at[mine, :], self_sem.at[k])
        keep.start()
        keep.wait()
        bulk = out.at[pl.ds(0, 3 * (DEVICES - 1)), :]
        pltpu.make_async_copy(bulk, bulk, recv_sem.at[k]).wait()

    exchange(out_1, in_1, 0)

    cos_t, sin_t = twist[0], twist[1]
    for c in range(3):
        both = table_left(lf_h[...], lf_l[...], in_1[pl.ds(c, DEVICES, stride=8), :])
        re, im = both[0:128], both[128:256]
        work[c, :, 0:128] = re * cos_t + im * sin_t
        work[c, :, 128:256] = im * cos_t - re * sin_t
    for c in range(3):
        work[c] = table_right(work[c], rf_h[...], rf_l[...])

    special = me < 2
    plain = jnp.where(special, 1.0, 0.0).astype(F32)
    turn = jnp.where(special, 0, 2 * lax.rem(me, 2) - 1).astype(F32)
    kz = jnp.where(me == 1, -64, me // 2).astype(F32)
    kz_top = jnp.where(me == 1, -64, 0).astype(F32)
    kz_low = jnp.where(me == 1, 0, me // 2).astype(F32)

    def signed(v):
        return jnp.where(v < GRID // 2, v, v - GRID)

    def stokes(i, carry):
        rows = pl.ds(pl.multiple_of(i * 16, 16), 16)
        f1 = lax.broadcasted_iota(jnp.int32, (16, 128), 0) + i * 16
        f2 = lax.broadcasted_iota(jnp.int32, (16, 128), 1)
        ix = signed(f1 // 16 + 8 * (f2 // 8))
        iy = signed(f1 % 16 + 16 * (f2 % 8))
        kx, ky = ix.astype(F32), iy.astype(F32)
        kx_top = jnp.where(ix == -64, kx, 0.0)
        ky_top = jnp.where(iy == -64, ky, 0.0)
        kx_low, ky_low = kx - kx_top, ky - ky_top
        square = kx * kx + ky * ky + kz * kz
        damping = (0.25 / GRID**3) * jnp.exp(square * (-((math.pi / GRID) ** 2)))
        inverse = 1.0 / jnp.maximum(square, 1.0)
        w_re, w_im = work[2, rows, 0:128], work[2, rows, 128:256]
        sides = (
            (work[0, rows, 0:128], work[1, rows, 0:128], plain * w_re - turn * w_im),
            (work[0, rows, 128:256], work[1, rows, 128:256], plain * w_im + turn * w_re),
        )
        done = []
        for u, v, w in sides:
            low = (kx_low * u + ky_low * v + kz_low * w) * inverse
            top = (kx_top * u + ky_top * v + kz_top * w) * inverse
            done.append(
                (
                    damping * (u - kx_low * low - kx_top * top),
                    damping * (v - ky_low * low - ky_top * top),
                    damping * (w - kz_low * low - kz_top * top),
                )
            )
        for c in range(2):
            work[c, rows, 0:128] = done[0][c]
            work[c, rows, 128:256] = done[1][c]
        work[2, rows, 0:128] = plain * done[0][2] + turn * done[1][2]
        work[2, rows, 128:256] = plain * done[1][2] - turn * done[0][2]
        return carry

    lax.fori_loop(0, 8, stokes, 0)

    for c in range(3):
        both = table_right(work[c], rb_h[...], rb_l[...])
        re, im = both[:, 0:128], both[:, 128:256]
        pair = jnp.concatenate([re * cos_t - im * sin_t, im * cos_t + re * sin_t], 0)
        out_2[pl.ds(c, DEVICES, stride=8), :] = table_left(lb_h[...], lb_l[...], pair)

    exchange(out_2, in_2, 1)

    for c in range(3):
        high, low = (zb_xy_h, zb_xy_l) if c < 2 else (zb_z_h, zb_z_l)
        grid[c] = table_left(high[...], low[...], in_2[pl.ds(c, DEVICES, stride=8), :])

    def gather(z, carry):
        rows = pl.ds(pl.multiple_of(z * 8, 8), 8)
        block = jnp.concatenate([grid[c, rows, :] for c in range(3)], 0)
        near_half = jnp.where(low_lane, block, 0.0)
        far_half = block - near_half
        both = jnp.concatenate([near_half, far_half], 0)
        top = narrow(both)
        first = mul(jnp.concatenate([top, both - top], 0).astype(BF16), plan_h[z])
        second = mul(top.astype(BF16), plan_l[z])
        sums = first[0:48] + first[48:96] + second
        for h in range(2):
            spot = pl.ds(pl.multiple_of((h * HALF + z) * 8, 8), 8)
            bz = depth[spot, :]
            for c in range(3):
                far[c, spot, :] = sums[h * 24 + c * 8 : h * 24 + c * 8 + 8] * bz
        return carry

    lax.fori_loop(0, HALF, gather, 0)

    for c in range(3):
        total = far[c, pl.ds(0, CELLS, stride=8), :]
        for g in range(1, CELL):
            total = total + far[c, pl.ds(g, CELLS, stride=8), :]
        spin[c] = near[c] + total * fill[...]

    for k in range(2):
        bulk = out_1.at[pl.ds(0, 3 * (DEVICES - 1)), :]
        pltpu.make_async_copy(bulk, bulk, send_sem.at[k]).wait()


def far_field(places, torques, near, fill):
    tables = [jnp.asarray(t) for t in make_tables()]
    vmem = pl.BlockSpec(memory_space=pltpu.VMEM)
    buffer = pltpu.VMEM((DEVICES * 8, 128), F32)
    return pl.pallas_call(
        far_kernel,
        name="far",
        out_shape=jax.ShapeDtypeStruct((3, CELLS, SLOT), F32),
        in_specs=[vmem] * (4 + len(tables)),
        out_specs=vmem,
        scratch_shapes=[
            pltpu.VMEM((3, GRID, 128), F32),
            pltpu.VMEM((HALF, 128, SLOT), BF16),
            pltpu.VMEM((HALF, 128, SLOT), BF16),
            pltpu.VMEM((CELLS * 8, SLOT), F32),
            buffer,
            buffer,
            buffer,
            buffer,
            pltpu.VMEM((3, 128, 256), F32),
            pltpu.VMEM((3, CELLS * 8, SLOT), F32),
            pltpu.SemaphoreType.DMA((2,)),
            pltpu.SemaphoreType.DMA((2,)),
            pltpu.SemaphoreType.DMA((2,)),
        ],
        compiler_params=pltpu.CompilerParams(collective_id=1, has_side_effects=True),
    )(places, torques, near, fill, *tables)


def shards(positions, torques, counts, neighbour_flags):
    shape = positions.shape
    flat = (3, CELLS, SLOT)
    torques = torques.reshape(flat)
    places, near, fill = near_field(positions.reshape(flat), torques, counts, neighbour_flags)
    spin = far_field(places, torques, near, fill)
    return places.reshape(shape), spin.reshape(shape)


def solution(mesh):
    in_specs = (
        P(None, "row", "col", None, None),
        P(None, "row", "col", None, None),
        P("row", "col", None),
        P(None, "row", "col", None),
    )
    out_specs = (P(None, "row", "col", None, None), P(None, "row", "col", None, None))
    return jax.shard_map(shards, mesh=mesh, in_specs=in_specs, out_specs=out_specs, check_vma=False)
```

time: 330 us -> 88.6 us (0.27); the launches traced: 325 us -> 88.3 us
  matrix products: 110 us -> 0 us
  Pallas kernels: 0 us -> 86.2 us
  other arithmetic: 56.5 us -> 0 us
  starting transfers between devices: 50.5 us -> 0 us
  local copies, waits for them, and re-layouts: 51.7 us -> 1.41 us
  waiting for transfers between devices: 43.7 us -> 0 us
  blocking collectives: 9.69 us -> 0 us
    dot_general x43 -> x0, matrix products: 110 us -> none  [the longest x21 71.5 us: pair_totals(): return jnp.einsum('nij,qnj->qni', weights, far_loads, precision=highest)]
    pallas_call x0 -> x2, Pallas kernels: none -> 86.2 us  [the longest x1 56.9 us: near_field(): pl.pallas_call(near_kernel, name='near', out_shape=(field, field, jax.Sha...]
    reduce_sum x3 -> x0, other arithmetic: 37.2 us -> none  [pair_totals(): jnp.sum(separation * separation, axis=0)]
    all_to_all x3 -> x0, starting transfers between devices: 26.8 us -> none  [the longest x1 15.4 us: solve_far(): lax.all_to_all(spectrum, 'col', split_axis=2, concat_axis=4, tiled=True)]
    ppermute x12 -> x0, starting transfers between devices: 23.6 us -> none  [the longest x6 15.9 us: with_halo(): lax.ppermute(lax.slice_in_dim(block, 0, width, axis=dim), axis, backward)]
    all_to_all x3 -> x0, waiting for transfers between devices: 22.5 us -> none  [the longest x1 8.82 us: solve_far(): lax.all_to_all(pencil, 'col', split_axis=4, concat_axis=2, tiled=True)]
    ppermute x12 -> x0, waiting for transfers between devices: 21.1 us -> none  [the longest x6 12.4 us: with_halo(): lax.ppermute(lax.slice_in_dim(block, block.shape[dim] - width, None, axis...]
    slice x100 -> x0, local copies, waits for them, and re-layouts: 14.4 us -> none  [the longest x7 4.61 us: near_field(): weight_total = weight_total + face_gate * totals[6]]
  transfers between devices with their start and end apart: 15 -> 0, of which waited for: 14 -> 0; matrix products, arithmetic and copies ran while one was open for 3% -> 0% of each run, Pallas kernels for 0% -> 0%
where the time goes in v1:
time: 88.6 us; the launch traced here: 88.3 us
  Pallas kernels  86.2 us (97%)
  local copies, waits for them, and re-layouts  1.41 us (2%)
    pallas_call x1, Pallas kernels, near_field(): pl.pallas_call(near_kernel, name='near', out_shape=(field, field, jax.Sha...  56.9 us
    pallas_call x1, Pallas kernels, far_field(): pl.pallas_call(far_kernel, name='far', out_shape=jax.ShapeDtypeStruct((3,...  29.4 us

profile of v1, /device:TPU:1, one launch (start us, length us, event | category | flops | bytes accessed | tf_op | source)
XLA Modules:
  0.0 88.3 jit_solution(12001238878396263330)
XLA Ops:
  0.6 56.9 %near.1 = (f32[3,32,128]{2,1,0:T(8,128)}, f32[3,32,128]{2,1,0:T(8,128)}, f32[32,128]{1,0:T(8,128)}) custom-call(f32[3,32,128]{2,1,0:T(8,128)} %bitcast.12, f32[3,32,128]{2,1,0:T(8,128)} %bitcast.8, s32[2,1,16]{2,1,0:T(1,128)} %cnt.1, s32[6,2,1,16]{3,2,1,0:T(1,128)} %flg.1), custom_call_target="tpu_custom_call" | custom-call | tf_op jit(solution)/shard_map/near/pallas_call | solution.py:278
  57.5 0.0 copy-start
  57.5 29.4 %far.1 = f32[3,32,128]{2,1,0:T(8,128)} custom-call(f32[3,32,128]{2,1,0:T(8,128)} %get-tuple-element.5.pos, f32[3,32,128]{2,1,0:T(8,128)} %bitcast.9, f32[3,32,128]{2,1,0:T(8,128)} %get-tuple-element.6.near, f32[32,128]{1,0:T(8,128)} %get-tuple-element.7.fill, bf16[128,128]{1,0:T(8,128)(2,1)} %constant.34.clone.zf_xy_h, ...), custom_call_target="tpu_custom_call" | custom-call | tf_op jit(solution)/shard_map/far/pallas_call | solution.py:551
  86.9 0.0 copy-done
  86.9 0.0 copy-start.1
  86.9 0.6 copy.27
  87.5 0.2 copy-done.1
  87.7 0.6 copy.28
Async XLA Ops:
  57.5 29.4 %copy-start = (f32[3,32,128]{2,1,0:T(8,128)S(1)}, f32[3,32,128]{2,1,0:T(8,128)}, u32[]{:S(2)}) copy-start(f32[3,32,128]{2,1,0:T(8,128)} %get-tuple-element.5.pos) | copy-start | bytes 147460
  86.9 0.8 copy-start.1

commit v2 on v1

--- a/solution.py
+++ b/solution.py
@@ -18,6 +18,7 @@
 CELLS = 32
 HALF = 16
 MESH = pl.DeviceIdType.MESH
+LOGICAL = pl.DeviceIdType.LOGICAL
 F32 = jnp.float32
 BF16 = jnp.bfloat16
 
@@ -27,9 +28,14 @@
 COUPLE = 0.5 / SLOT
 MID = 0.5 * CELL
 
-A_ROWS = 48
+A_ROWS = 32
+GROUP = SLOT // A_ROWS
 B_ROWS = 16
 L_ROWS = 16
+A_PITCH = A_ROWS + 1
+B_PITCH = B_ROWS + 1
+L_PITCH = L_ROWS + 1
+T_PITCH = 9
 
 
 def narrow(v):
@@ -48,48 +54,47 @@
 
 
 def put_receiver(afeat, half, px, py, pz):
-    base = half * HALF * A_ROWS
+    base = half * HALF * A_PITCH
 
     def row(k, v):
-        afeat[pl.ds(base + k, HALF, stride=A_ROWS), :] = v
-
-    parts = [split3(v * (2.0 * KAPPA)) for v in (px, py, pz)]
+        afeat[pl.ds(base + k, HALF, stride=A_PITCH), :] = v
+
     size = split3(-KAPPA * (px * px + py * py + pz * pz))
-    for d in range(3):
-        h, m, l = parts[d]
+    for d, v in enumerate((px, py, pz)):
+        h, m, l = split3(v * (2.0 * KAPPA))
         row(d, h)
         row(8 + d, h)
         row(11 + d, h)
+        row((7, 14, 15)[d], l)
         row(16 + d, m)
         row(24 + d, m)
-        row(32 + d, l)
     row(6, size[0])
     row(16 + 6, size[1])
-    row(32 + 6, size[2])
 
 
 def put_source(bfeat, lfeat, slot, half, place, torque, fill, shift, gate):
     place = [place[d] + shift[d] if shift[d] != 0.0 else place[d] for d in range(3)]
     x, y, z = place
-    base = half * HALF * B_ROWS
+    base = half * HALF * B_PITCH
     for d in range(3):
         h, m, l = split3(place[d])
-        put(bfeat, slot, base + d, B_ROWS, h)
-        put(bfeat, slot, base + 8 + d, B_ROWS, m)
-        put(bfeat, slot, base + 11 + d, B_ROWS, l)
+        put(bfeat, slot, base + d, B_PITCH, h)
+        put(bfeat, slot, base + 8 + d, B_PITCH, m)
+        put(bfeat, slot, base + 11 + d, B_PITCH, l)
+        put(bfeat, slot, base + (7, 14, 15)[d], B_PITCH, h)
     for k, v in enumerate(split3(-KAPPA * (x * x + y * y + z * z))):
-        put(bfeat, slot, base + 3 + k, B_ROWS, v)
+        put(bfeat, slot, base + 3 + k, B_PITCH, v)
     if gate is not None:
         torque = [t * gate for t in torque]
         fill = fill * gate
     tx, ty, tz = torque
     loads = (tx, ty, tz, ty * z - tz * y, tz * x - tx * z, tx * y - ty * x)
-    base = half * HALF * L_ROWS
+    base = half * HALF * L_PITCH
     for q, v in enumerate(loads):
         h = narrow(v)
-        put(lfeat, slot, base + q, L_ROWS, h)
-        put(lfeat, slot, base + 8 + q, L_ROWS, v - h)
-    put(lfeat, slot, base + 6, L_ROWS, fill)
+        put(lfeat, slot, base + q, L_PITCH, h)
+        put(lfeat, slot, base + 8 + q, L_PITCH, v - h)
+    put(lfeat, slot, base + 6, L_PITCH, fill)
 
 
 def near_kernel(
@@ -154,43 +159,51 @@
 
     one = jnp.ones((CELLS, SLOT), F32)
     zero = jnp.zeros((CELLS, SLOT), F32)
-    for k in (7, 14, 15, 19, 20, 21, 23, 27, 28, 29, 30, 31, 35, 36, 37, 39, *range(40, 48)):
-        afeat[pl.ds(k, CELLS, stride=A_ROWS), :] = zero
+    for k in (19, 20, 21, 23, 27, 28, 29, 30, 31):
+        afeat[pl.ds(k, CELLS, stride=A_PITCH), :] = zero
     for k in (3, 4, 5):
-        afeat[pl.ds(k, CELLS, stride=A_ROWS), :] = one
+        afeat[pl.ds(k, CELLS, stride=A_PITCH), :] = one
     for e in range(7):
-        put(bfeat, e, 6, B_ROWS, one)
+        put(bfeat, e, 6, B_PITCH, one)
         for k in (7, 14, 15):
-            put(bfeat, e, k, B_ROWS, zero)
-        for k in (7, 14, 15):
-            put(lfeat, e, k, L_ROWS, zero)
-
-    def weighted(at, cell, faces):
-        def wide(ref, n):
-            blocks = [ref[e, pl.ds(pl.multiple_of(cell * n, n), n), :] for e in faces]
-            return (blocks[0] if len(blocks) == 1 else jnp.concatenate(blocks, 1)).astype(BF16)
-
-        b = wide(bfeat, B_ROWS)
-        b = jnp.concatenate([b, b, b], 0)
-        power = jnp.dot(at, b, preferred_element_type=F32)
-        w = jnp.exp2(power).astype(BF16)
-        return lax.dot_general(wide(lfeat, L_ROWS), w, (((1,), (1,)), ((), ())), preferred_element_type=F32)
-
-    def inner_faces(z, carry):
-        for h in range(2):
-            cell = h * HALF + z
-            at = afeat[pl.ds(pl.multiple_of(cell * A_ROWS, A_ROWS), A_ROWS), :].T.astype(BF16)
-            trans[cell] = at
-            acc = weighted(at, cell, (0, 1)) + weighted(at, cell, (2, 3))
-            totals[pl.ds(pl.multiple_of(cell * 8, 8), 8), :] = acc[0:8] + acc[8:16]
+            put(lfeat, e, k, L_PITCH, zero)
+
+    owner = lax.broadcasted_iota(jnp.int32, (SLOT, SLOT), 1) // A_ROWS
+
+    def wide(ref, n, cell, faces):
+        blocks = [ref[e, pl.ds(cell * (n + 1), n), :] for e in faces]
+        return (blocks[0] if len(blocks) == 1 else jnp.concatenate(blocks, 1)).astype(BF16)
+
+    def weighted(block, first, pairs):
+        ats = [jnp.where(owner == k, block, jnp.zeros_like(block)) for k in range(GROUP)]
+        acc = [None] * GROUP
+        for faces in pairs:
+            b = []
+            for k in range(GROUP):
+                part = wide(bfeat, B_ROWS, first + k, faces)
+                b += [part, part]
+            b = jnp.concatenate(b, 0)
+            power = jnp.dot(jnp.concatenate(ats, 0), b, preferred_element_type=F32)
+            for k in range(GROUP):
+                w = jnp.exp2(power[k * SLOT : (k + 1) * SLOT]).astype(BF16)
+                load = wide(lfeat, L_ROWS, first + k, faces)
+                out = lax.dot_general(load, w, (((1,), (1,)), ((), ())), preferred_element_type=F32)
+                acc[k] = out if acc[k] is None else acc[k] + out
+        return acc
+
+    def inner_faces(i, carry):
+        first = i * GROUP
+        rows = [afeat[pl.ds((first + k) * A_PITCH, A_ROWS), :] for k in range(GROUP)]
+        block = jnp.concatenate(rows, 0).T.astype(BF16)
+        trans[i] = block
+        for k, acc in enumerate(weighted(block, first, ((0, 1, 2, 3),))):
+            totals[pl.ds((first + k) * T_PITCH, 8), :] = acc[0:8] + acc[8:16]
         return carry
 
-    def outer_faces(z, carry):
-        for h in range(2):
-            cell = h * HALF + z
-            at = trans[cell]
-            acc = weighted(at, cell, (4, 5)) + weighted(at, cell, (6,))
-            spot = pl.ds(pl.multiple_of(cell * 8, 8), 8)
+    def outer_faces(i, carry):
+        first = i * GROUP
+        for k, acc in enumerate(weighted(trans[i], first, ((4, 5, 6),))):
+            spot = pl.ds((first + k) * T_PITCH, 8)
             totals[spot, :] = totals[spot, :] + (acc[0:8] + acc[8:16])
         return carry
 
@@ -223,7 +236,7 @@
                 (float(CELL) if h == 0 else -float(CELL), 0.0, 0.0),
                 gates[0 if h == 0 else 1, part, :],
             )
-        lax.fori_loop(0, HALF, inner_faces, 0)
+        lax.fori_loop(0, CELLS // GROUP, inner_faces, 0)
         for copy in copies:
             copy.wait_recv()
         for h in range(2):
@@ -247,9 +260,9 @@
                     (0.0, float(lift), 0.0),
                     gates[face, part, :],
                 )
-        lax.fori_loop(0, HALF, outer_faces, 0)
-
-        tot = [totals[pl.ds(q, CELLS, stride=8), :] for q in range(7)]
+        lax.fori_loop(0, CELLS // GROUP, outer_faces, 0)
+
+        tot = [totals[pl.ds(q, CELLS, stride=T_PITCH), :] for q in range(7)]
         fill = state[6]
         x, y, z = (here[d] for d in range(3))
         speed = (
@@ -285,11 +298,11 @@
             pltpu.VMEM((7, CELLS, SLOT), F32),
             pltpu.VMEM((STEPS - 1, 3, CELLS, SLOT), F32),
             pltpu.VMEM((6, CELLS, SLOT), F32),
-            pltpu.VMEM((CELLS * A_ROWS, SLOT), F32),
-            pltpu.VMEM((CELLS, SLOT, A_ROWS), BF16),
-            pltpu.VMEM((7, CELLS * B_ROWS, SLOT), F32),
-            pltpu.VMEM((7, CELLS * L_ROWS, SLOT), F32),
-            pltpu.VMEM((CELLS * 8, SLOT), F32),
+            pltpu.VMEM((CELLS * A_PITCH, SLOT), F32),
+            pltpu.VMEM((CELLS // GROUP, SLOT, SLOT), BF16),
+            pltpu.VMEM((7, CELLS * B_PITCH, SLOT), F32),
+            pltpu.VMEM((7, CELLS * L_PITCH, SLOT), F32),
+            pltpu.VMEM((CELLS * T_PITCH, SLOT), F32),
             pltpu.VMEM((2, 7, HALF, SLOT), F32),
             pltpu.VMEM((2, 7, CELLS, SLOT), F32),
             pltpu.VMEM((STEPS - 1, 2, 3, HALF, SLOT), F32),
@@ -376,14 +389,14 @@
     barrier = pltpu.get_barrier_semaphore()
 
     def peer(k):
-        p = lax.rem(me + k, DEVICES)
-        return p, (p // COLS, lax.rem(p, COLS))
+        p = me + k
+        return jnp.where(p >= DEVICES, p - DEVICES, p)
 
     def greet(k, carry):
-        pl.semaphore_signal(barrier, inc=1, device_id=peer(k)[1], device_id_type=MESH)
+        pl.semaphore_signal(barrier, inc=1, device_id=peer(k), device_id_type=LOGICAL)
         return carry
 
-    lax.fori_loop(1, DEVICES, greet, 0)
+    lax.fori_loop(1, DEVICES, greet, 0, unroll=9)
 
     level = lax.broadcasted_iota(jnp.int32, (CELL, SLOT), 0).astype(F32) + 0.5
     low_lane = lax.broadcasted_iota(jnp.int32, (24, SLOT), 1) < 64
@@ -424,18 +437,18 @@
 
     def exchange(out, into, k):
         def post(i, carry):
-            p, where = peer(i)
+            p = peer(i)
             pltpu.make_async_remote_copy(
                 src_ref=out.at[pl.ds(pl.multiple_of(p * 8, 8), 3), :],
                 dst_ref=into.at[pl.ds(pl.multiple_of(me * 8, 8), 3), :],
                 send_sem=send_sem.at[k],
                 recv_sem=recv_sem.at[k],
-                device_id=where,
-                device_id_type=MESH,
+                device_id=p,
+                device_id_type=LOGICAL,
             ).start()
             return carry
 
-        lax.fori_loop(1, DEVICES, post, 0)
+        lax.fori_loop(1, DEVICES, post, 0, unroll=9)
         mine = pl.ds(pl.multiple_of(me * 8, 8), 3)
         keep = pltpu.make_async_copy(out.at[mine, :], into.at[mine, :], self_sem.at[k])
         keep.start()

time: 88.6 us -> 64.3 us (0.73)
  Pallas kernels: 86.2 us -> 61.9 us
    pallas_call x1, Pallas kernels: 56.9 us -> 33.6 us  [near_field(): pl.pallas_call(near_kernel, name='near', out_shape=(field, field, jax.Sha...]
    pallas_call x1, Pallas kernels: 29.4 us -> 28.3 us  [far_field(): pl.pallas_call(far_kernel, name='far', out_shape=jax.ShapeDtypeStruct((3,...]
where the time goes in v2:
time: 64.3 us; the launch traced here: 64 us
  Pallas kernels  61.9 us (96%)
  local copies, waits for them, and re-layouts  1.41 us (2%)
  between operations  0.67 us (1%)
    pallas_call x1, Pallas kernels, near_field(): pl.pallas_call(near_kernel, name='near', out_shape=(field, field, jax.Sha...  33.6 us
    pallas_call x1, Pallas kernels, far_field(): pl.pallas_call(far_kernel, name='far', out_shape=jax.ShapeDtypeStruct((3,...  28.3 us
    unnamed x6, local copies, waits for them, and re-layouts  1.41 us

profile of v2, /device:TPU:1, one launch (start us, length us, event | category | flops | bytes accessed | tf_op | source)
XLA Modules:
  0.0 64.0 jit_solution(12628960720360451492)
XLA Ops:
  0.6 33.6 %near.1 = (f32[3,32,128]{2,1,0:T(8,128)}, f32[3,32,128]{2,1,0:T(8,128)}, f32[32,128]{1,0:T(8,128)}) custom-call(f32[3,32,128]{2,1,0:T(8,128)} %bitcast.12, f32[3,32,128]{2,1,0:T(8,128)} %bitcast.8, s32[2,1,16]{2,1,0:T(1,128)} %cnt.1, s32[6,2,1,16]{3,2,1,0:T(1,128)} %flg.1), custom_call_target="tpu_custom_call" | custom-call | tf_op jit(solution)/shard_map/near/pallas_call | solution.py:291
  34.2 0.0 copy-start
  34.2 28.3 %far.1 = f32[3,32,128]{2,1,0:T(8,128)} custom-call(f32[3,32,128]{2,1,0:T(8,128)} %get-tuple-element.5.pos, f32[3,32,128]{2,1,0:T(8,128)} %bitcast.9, f32[3,32,128]{2,1,0:T(8,128)} %get-tuple-element.6.near, f32[32,128]{1,0:T(8,128)} %get-tuple-element.7.fill, bf16[128,128]{1,0:T(8,128)(2,1)} %constant.34.clone.zf_xy_h, ...), custom_call_target="tpu_custom_call" | custom-call | tf_op jit(solution)/shard_map/far/pallas_call | solution.py:564
  62.6 0.0 copy-done
  62.6 0.0 copy-start.1
  62.6 0.6 copy.27
  63.2 0.2 copy-done.1
  63.4 0.6 copy.28
Async XLA Ops:
  34.2 28.4 %copy-start = (f32[3,32,128]{2,1,0:T(8,128)S(1)}, f32[3,32,128]{2,1,0:T(8,128)}, u32[]{:S(2)}) copy-start(f32[3,32,128]{2,1,0:T(8,128)} %get-tuple-element.5.pos) | copy-start | bytes 147460
  62.6 0.8 %copy-start.1 = (f32[3,32,128]{2,1,0:T(8,128)S(1)}, f32[3,32,128]{2,1,0:T(8,128)}, u32[]{:S(2)}) copy-start(f32[3,32,128]{2,1,0:T(8,128)} %far.1) | copy-start | bytes 147460

commit v3 on v2

--- a/solution.py
+++ b/solution.py
@@ -36,6 +36,66 @@
 B_PITCH = B_ROWS + 1
 L_PITCH = L_ROWS + 1
 T_PITCH = 9
+
+
+def halves(table):
+    high = table.astype(np.float32).astype(jnp.bfloat16)
+    low = (table - high.astype(np.float64)).astype(np.float32).astype(jnp.bfloat16)
+    return high, low
+
+
+def make_tables():
+    n = np.arange(GRID)
+    level = np.where(n == 1, 64, n // 2)
+    angle = 2.0 * np.pi * (level[:, None] * n[None, :] % GRID) / GRID
+    cosine, sine = np.cos(angle), np.sin(angle)
+    even = (n % 2 == 0)[:, None]
+    whole = (n < 2)[:, None]
+    basis_xy = np.where(whole | even, cosine, sine)
+    basis_z = np.where(whole | ~even, cosine, sine)
+    count = np.where(n < 2, 1.0, 2.0)[:, None]
+    back_xy, back_z = (basis_xy * count).T, (basis_z * count).T
+
+    def wave(a, b, period_a, period_b):
+        return 2.0 * np.pi * ((a * b[0] % period_a) / period_a + (b[1] % period_b) / period_b)
+
+    r, q = n // 16, n % 16
+    turn_l = 2.0 * np.pi * ((r[:, None] * r[None, :] % 8) / 8 + (q[:, None] * q[None, :] % 16) / 16)
+    s, t = n // 8, n % 8
+    turn_r = 2.0 * np.pi * ((s[:, None] * s[None, :] % 16) / 16 + (t[:, None] * t[None, :] % 8) / 8)
+    twist = 2.0 * np.pi * (r[:, None] * s[None, :] + q[:, None] * t[None, :]) / GRID
+    cl, sl = np.cos(turn_l), np.sin(turn_l)
+    cr, sr = np.cos(turn_r), np.sin(turn_r)
+    left = np.concatenate([cl, -sl], 0)
+    left_back = np.concatenate([cl, -sl], 1)
+    right = np.block([[cr, -sr], [sr, cr]])
+    right_back = np.block([[cr, sr], [-sr, cr]])
+    along_z = [half for table in (basis_xy, basis_z, back_xy, back_z) for half in halves(table)]
+    out = [np.stack(along_z)] + [np.stack(halves(table)) for table in (left, left_back, right, right_back)]
+    return out + [np.stack([np.cos(twist), np.sin(twist)]).astype(np.float32)]
+
+
+def cut(v):
+    h = v.astype(BF16)
+    return h, (v - h.astype(F32)).astype(BF16)
+
+
+def mul(a, b):
+    return jnp.dot(a, b, preferred_element_type=F32)
+
+
+def mul_t(a, b):
+    return lax.dot_general(a, b, (((1,), (1,)), ((), ())), preferred_element_type=F32)
+
+
+def table_left(high, low, v):
+    vh, vl = cut(v)
+    return mul(high, vh) + (mul(low, vh) + mul(high, vl))
+
+
+def table_right(v, high, low):
+    vh, vl = cut(v)
+    return mul(vh, high) + (mul(vl, high) + mul(vh, low))
 
 
 def narrow(v):
@@ -97,10 +157,12 @@
     put(lfeat, slot, base + 6, L_PITCH, fill)
 
 
-def near_kernel(
-    pos_in, tor_in, cnt, flg, pos_out, near_out, fill_out,
-    state, places, gates, afeat, trans, bfeat, lfeat, totals,
-    full_x, full_y, part_x, part_y, send_sem, recv_sem,
+def kernel(
+    pos_in, tor_in, cnt, flg, z_far, lf_far, lb_far, rf_far, rb_far, twist_far, pos_out, spin,
+    near_out, state, places, gates, afeat, trans, bfeat, lfeat, totals,
+    full_x, full_y, part_x, part_y, send_sem, recv_sem, tell,
+    z_tab, lf, lb, rf, rb, twist, table_sem,
+    grid, plan_h, plan_l, depth, out_1, in_1, out_2, in_2, work, far, all_send, all_recv, self_sem,
 ):
     row = lax.axis_index("row")
     col = lax.axis_index("col")
@@ -114,6 +176,30 @@
     for peer in peers:
         pl.semaphore_signal(barrier, inc=1, device_id=peer, device_id_type=MESH)
 
+    tables = [
+        pltpu.make_async_copy(src, dst, table_sem.at[k])
+        for k, (src, dst) in enumerate(
+            ((z_far, z_tab), (lf_far, lf), (lb_far, lb), (rf_far, rf), (rb_far, rb), (twist_far, twist))
+        )
+    ]
+    for table in tables:
+        table.start()
+
+    def inform(k, steps):
+        for down, right in steps:
+            where = (lax.rem(row + down + ROWS, ROWS), lax.rem(col + right + COLS, COLS))
+            pl.semaphore_signal(tell.at[k], inc=1, device_id=where, device_id_type=MESH)
+
+    def learn(step):
+        if step == 0:
+            inform(0, ((2, 0), (-2, 0), (0, 2), (0, -2)))
+        elif step == 1:
+            pl.semaphore_wait(tell.at[0], 4)
+            inform(1, ((0, 4), (0, -4)))
+        else:
+            pl.semaphore_wait(tell.at[1], 2)
+            inform(2, [(k, 0) for k in range(1, ROWS)])
+
     lane = lax.broadcasted_iota(jnp.int32, (1, SLOT), 1)
 
     def spread_scalars(z, carry):
@@ -125,7 +211,6 @@
 
     lax.fori_loop(0, HALF, spread_scalars, 0)
     fill = state[6]
-    fill_out[...] = fill
     for d in range(3):
         state[d] = pos_in[d] - MID
         state[3 + d] = tor_in[d] * fill
@@ -239,6 +324,7 @@
         lax.fori_loop(0, CELLS // GROUP, inner_faces, 0)
         for copy in copies:
             copy.wait_recv()
+        learn(step)
         for h in range(2):
             part = slice(h * HALF, (h + 1) * HALF)
             near_x = full_x if step == 0 else part_x.at[step - 1]
@@ -279,130 +365,20 @@
                 torque = tor_in[d]
                 near_out[d] = (torque + COUPLE * (tot[d] - tot[6] * torque)) * fill
 
-    for step in range(STEPS):
-        for copy in halo(step):
-            copy.wait_send()
-
-
-def near_field(positions, torques, counts, flags):
-    vmem = pl.BlockSpec(memory_space=pltpu.VMEM)
-    smem = pl.BlockSpec(memory_space=pltpu.SMEM)
-    field = jax.ShapeDtypeStruct((3, CELLS, SLOT), F32)
-    return pl.pallas_call(
-        near_kernel,
-        name="near",
-        out_shape=(field, field, jax.ShapeDtypeStruct((CELLS, SLOT), F32)),
-        in_specs=[vmem, vmem, smem, smem],
-        out_specs=(vmem, vmem, vmem),
-        scratch_shapes=[
-            pltpu.VMEM((7, CELLS, SLOT), F32),
-            pltpu.VMEM((STEPS - 1, 3, CELLS, SLOT), F32),
-            pltpu.VMEM((6, CELLS, SLOT), F32),
-            pltpu.VMEM((CELLS * A_PITCH, SLOT), F32),
-            pltpu.VMEM((CELLS // GROUP, SLOT, SLOT), BF16),
-            pltpu.VMEM((7, CELLS * B_PITCH, SLOT), F32),
-            pltpu.VMEM((7, CELLS * L_PITCH, SLOT), F32),
-            pltpu.VMEM((CELLS * T_PITCH, SLOT), F32),
-            pltpu.VMEM((2, 7, HALF, SLOT), F32),
-            pltpu.VMEM((2, 7, CELLS, SLOT), F32),
-            pltpu.VMEM((STEPS - 1, 2, 3, HALF, SLOT), F32),
-            pltpu.VMEM((STEPS - 1, 2, 3, CELLS, SLOT), F32),
-            pltpu.SemaphoreType.DMA((STEPS, 4)),
-            pltpu.SemaphoreType.DMA((STEPS, 4)),
-        ],
-        compiler_params=pltpu.CompilerParams(collective_id=0, has_side_effects=True),
-    )(positions, torques, counts, flags)
-
-
-def halves(table):
-    high = table.astype(np.float32).astype(jnp.bfloat16)
-    low = (table - high.astype(np.float64)).astype(np.float32).astype(jnp.bfloat16)
-    return high, low
-
-
-def make_tables():
-    n = np.arange(GRID)
-    level = np.where(n == 1, 64, n // 2)
-    angle = 2.0 * np.pi * (level[:, None] * n[None, :] % GRID) / GRID
-    cosine, sine = np.cos(angle), np.sin(angle)
-    even = (n % 2 == 0)[:, None]
-    whole = (n < 2)[:, None]
-    basis_xy = np.where(whole | even, cosine, sine)
-    basis_z = np.where(whole | ~even, cosine, sine)
-    count = np.where(n < 2, 1.0, 2.0)[:, None]
-    back_xy, back_z = (basis_xy * count).T, (basis_z * count).T
-
-    def wave(a, b, period_a, period_b):
-        return 2.0 * np.pi * ((a * b[0] % period_a) / period_a + (b[1] % period_b) / period_b)
-
-    r, q = n // 16, n % 16
-    turn_l = 2.0 * np.pi * ((r[:, None] * r[None, :] % 8) / 8 + (q[:, None] * q[None, :] % 16) / 16)
-    s, t = n // 8, n % 8
-    turn_r = 2.0 * np.pi * ((s[:, None] * s[None, :] % 16) / 16 + (t[:, None] * t[None, :] % 8) / 8)
-    twist = 2.0 * np.pi * (r[:, None] * s[None, :] + q[:, None] * t[None, :]) / GRID
-    cl, sl = np.cos(turn_l), np.sin(turn_l)
-    cr, sr = np.cos(turn_r), np.sin(turn_r)
-    left = np.concatenate([cl, -sl], 0)
-    left_back = np.concatenate([cl, -sl], 1)
-    right = np.block([[cr, -sr], [sr, cr]])
-    right_back = np.block([[cr, sr], [-sr, cr]])
-    out = []
-    for table in (basis_xy, basis_z, back_xy, back_z, left, left_back, right, right_back):
-        high, low = halves(table)
-        out += [high, low]
-    out.append(np.stack([np.cos(twist), np.sin(twist)]).astype(np.float32))
-    return out
-
-
-def cut(v):
-    h = v.astype(BF16)
-    return h, (v - h.astype(F32)).astype(BF16)
-
-
-def mul(a, b):
-    return jnp.dot(a, b, preferred_element_type=F32)
-
-
-def mul_t(a, b):
-    return lax.dot_general(a, b, (((1,), (1,)), ((), ())), preferred_element_type=F32)
-
-
-def table_left(high, low, v):
-    vh, vl = cut(v)
-    return mul(high, vh) + (mul(low, vh) + mul(high, vl))
-
-
-def table_right(v, high, low):
-    vh, vl = cut(v)
-    return mul(vh, high) + (mul(vl, high) + mul(vh, low))
-
-
-def far_kernel(
-    pos, tor, near, fill, zf_xy_h, zf_xy_l, zf_z_h, zf_z_l, zb_xy_h, zb_xy_l, zb_z_h, zb_z_l,
-    lf_h, lf_l, lb_h, lb_l, rf_h, rf_l, rb_h, rb_l, twist,
-    spin,
-    grid, plan_h, plan_l, depth, out_1, in_1, out_2, in_2, work, far, send_sem, recv_sem, self_sem,
-):
-    row = lax.axis_index("row")
-    col = lax.axis_index("col")
     me = row * COLS + col
-    barrier = pltpu.get_barrier_semaphore()
 
     def peer(k):
         p = me + k
         return jnp.where(p >= DEVICES, p - DEVICES, p)
 
-    def greet(k, carry):
-        pl.semaphore_signal(barrier, inc=1, device_id=peer(k), device_id_type=LOGICAL)
-        return carry
-
-    lax.fori_loop(1, DEVICES, greet, 0, unroll=9)
-
     level = lax.broadcasted_iota(jnp.int32, (CELL, SLOT), 0).astype(F32) + 0.5
     low_lane = lax.broadcasted_iota(jnp.int32, (24, SLOT), 1) < 64
 
+    for table in tables:
+        table.wait()
+
     def bins(d, cell):
-        apart = pos[d, pl.ds(cell, 1), :] - level
+        apart = pos_out[d, pl.ds(cell, 1), :] - level
         return jnp.exp(-apart * apart)
 
     def spread(z, carry):
@@ -412,7 +388,7 @@
             bx, by, bz = (bins(d, cell) for d in range(3))
             depth[pl.ds(pl.multiple_of(cell * 8, 8), 8), :] = bz
             planar += [bx[a : a + 1, :] * by for a in range(CELL)]
-            lift = [tor[c, pl.ds(cell, 1), :] * fill[pl.ds(cell, 1), :] * bz for c in range(3)]
+            lift = [state[3 + c, pl.ds(cell, 1), :] * bz for c in range(3)]
             top = [narrow(v) for v in lift]
             lifted += top
             rest += [v - t for v, t in zip(lift, top)]
@@ -430,10 +406,10 @@
     lax.fori_loop(0, HALF, spread, 0)
 
     for c in range(3):
-        high, low = (zf_xy_h, zf_xy_l) if c < 2 else (zf_z_h, zf_z_l)
-        out_1[pl.ds(c, DEVICES, stride=8), :] = table_left(high[...], low[...], grid[c])
-
-    pl.semaphore_wait(barrier, DEVICES - 1)
+        n = 0 if c < 2 else 2
+        out_1[pl.ds(c, DEVICES, stride=8), :] = table_left(z_tab[n], z_tab[n + 1], grid[c])
+
+    pl.semaphore_wait(tell.at[2], ROWS - 1)
 
     def exchange(out, into, k):
         def post(i, carry):
@@ -441,8 +417,8 @@
             pltpu.make_async_remote_copy(
                 src_ref=out.at[pl.ds(pl.multiple_of(p * 8, 8), 3), :],
                 dst_ref=into.at[pl.ds(pl.multiple_of(me * 8, 8), 3), :],
-                send_sem=send_sem.at[k],
-                recv_sem=recv_sem.at[k],
+                send_sem=all_send.at[k],
+                recv_sem=all_recv.at[k],
                 device_id=p,
                 device_id_type=LOGICAL,
             ).start()
@@ -454,18 +430,18 @@
         keep.start()
         keep.wait()
         bulk = out.at[pl.ds(0, 3 * (DEVICES - 1)), :]
-        pltpu.make_async_copy(bulk, bulk, recv_sem.at[k]).wait()
+        pltpu.make_async_copy(bulk, bulk, all_recv.at[k]).wait()
 
     exchange(out_1, in_1, 0)
 
     cos_t, sin_t = twist[0], twist[1]
     for c in range(3):
-        both = table_left(lf_h[...], lf_l[...], in_1[pl.ds(c, DEVICES, stride=8), :])
+        both = table_left(lf[0], lf[1], in_1[pl.ds(c, DEVICES, stride=8), :])
         re, im = both[0:128], both[128:256]
         work[c, :, 0:128] = re * cos_t + im * sin_t
         work[c, :, 128:256] = im * cos_t - re * sin_t
     for c in range(3):
-        work[c] = table_right(work[c], rf_h[...], rf_l[...])
+        work[c] = table_right(work[c], rf[0], rf[1])
 
     special = me < 2
     plain = jnp.where(special, 1.0, 0.0).astype(F32)
@@ -516,16 +492,16 @@
     lax.fori_loop(0, 8, stokes, 0)
 
     for c in range(3):
-        both = table_right(work[c], rb_h[...], rb_l[...])
+        both = table_right(work[c], rb[0], rb[1])
         re, im = both[:, 0:128], both[:, 128:256]
         pair = jnp.concatenate([re * cos_t - im * sin_t, im * cos_t + re * sin_t], 0)
-        out_2[pl.ds(c, DEVICES, stride=8), :] = table_left(lb_h[...], lb_l[...], pair)
+        out_2[pl.ds(c, DEVICES, stride=8), :] = table_left(lb[0], lb[1], pair)
 
     exchange(out_2, in_2, 1)
 
     for c in range(3):
-        high, low = (zb_xy_h, zb_xy_l) if c < 2 else (zb_z_h, zb_z_l)
-        grid[c] = table_left(high[...], low[...], in_2[pl.ds(c, DEVICES, stride=8), :])
+        n = 4 if c < 2 else 6
+        grid[c] = table_left(z_tab[n], z_tab[n + 1], in_2[pl.ds(c, DEVICES, stride=8), :])
 
     def gather(z, carry):
         rows = pl.ds(pl.multiple_of(z * 8, 8), 8)
@@ -550,24 +526,49 @@
         total = far[c, pl.ds(0, CELLS, stride=8), :]
         for g in range(1, CELL):
             total = total + far[c, pl.ds(g, CELLS, stride=8), :]
-        spin[c] = near[c] + total * fill[...]
+        spin[c] = near_out[c] + total * state[6]
 
     for k in range(2):
         bulk = out_1.at[pl.ds(0, 3 * (DEVICES - 1)), :]
-        pltpu.make_async_copy(bulk, bulk, send_sem.at[k]).wait()
-
-
-def far_field(places, torques, near, fill):
+        pltpu.make_async_copy(bulk, bulk, all_send.at[k]).wait()
+    for step in range(STEPS):
+        for copy in halo(step):
+            copy.wait_send()
+def shards(positions, torques, counts, neighbour_flags):
+    shape = positions.shape
+    flat = (3, CELLS, SLOT)
     tables = [jnp.asarray(t) for t in make_tables()]
     vmem = pl.BlockSpec(memory_space=pltpu.VMEM)
+    smem = pl.BlockSpec(memory_space=pltpu.SMEM)
+    field = jax.ShapeDtypeStruct(flat, F32)
     buffer = pltpu.VMEM((DEVICES * 8, 128), F32)
-    return pl.pallas_call(
-        far_kernel,
-        name="far",
-        out_shape=jax.ShapeDtypeStruct((3, CELLS, SLOT), F32),
-        in_specs=[vmem] * (4 + len(tables)),
-        out_specs=vmem,
+    places, spin = pl.pallas_call(
+        kernel,
+        name="spinners",
+        out_shape=(field, field),
+        in_specs=[vmem, vmem, smem, smem] + [pl.BlockSpec(memory_space=pl.ANY)] * len(tables),
+        out_specs=(vmem, vmem),
         scratch_shapes=[
+            pltpu.VMEM(flat, F32),
+            pltpu.VMEM((7, CELLS, SLOT), F32),
+            pltpu.VMEM((STEPS - 1, 3, CELLS, SLOT), F32),
+            pltpu.VMEM((6, CELLS, SLOT), F32),
+            pltpu.VMEM((CELLS * A_PITCH, SLOT), F32),
+            pltpu.VMEM((CELLS // GROUP, SLOT, SLOT), BF16),
+            pltpu.VMEM((7, CELLS * B_PITCH, SLOT), F32),
+            pltpu.VMEM((7, CELLS * L_PITCH, SLOT), F32),
+            pltpu.VMEM((CELLS * T_PITCH, SLOT), F32),
+            pltpu.VMEM((2, 7, HALF, SLOT), F32),
+            pltpu.VMEM((2, 7, CELLS, SLOT), F32),
+            pltpu.VMEM((STEPS - 1, 2, 3, HALF, SLOT), F32),
+            pltpu.VMEM((STEPS - 1, 2, 3, CELLS, SLOT), F32),
+            pltpu.SemaphoreType.DMA((STEPS, 4)),
+            pltpu.SemaphoreType.DMA((STEPS, 4)),
+            pltpu.SemaphoreType.REGULAR((3,)),
+        ]
+        + [pltpu.VMEM(t.shape, t.dtype) for t in tables]
+        + [
+            pltpu.SemaphoreType.DMA((len(tables),)),
             pltpu.VMEM((3, GRID, 128), F32),
             pltpu.VMEM((HALF, 128, SLOT), BF16),
             pltpu.VMEM((HALF, 128, SLOT), BF16),
@@ -582,16 +583,8 @@
             pltpu.SemaphoreType.DMA((2,)),
             pltpu.SemaphoreType.DMA((2,)),
         ],
-        compiler_params=pltpu.CompilerParams(collective_id=1, has_side_effects=True),
-    )(places, torques, near, fill, *tables)
-
-
-def shards(positions, torques, counts, neighbour_flags):
-    shape = positions.shape
-    flat = (3, CELLS, SLOT)
-    torques = torques.reshape(flat)
-    places, near, fill = near_field(positions.reshape(flat), torques, counts, neighbour_flags)
-    spin = far_field(places, torques, near, fill)
+        compiler_params=pltpu.CompilerParams(collective_id=0, has_side_effects=True),
+    )(positions.reshape(flat), torques.reshape(flat), counts, neighbour_flags, *tables)
     return places.reshape(shape), spin.reshape(shape)
 
 

time: 64.3 us -> 61.8 us (0.961)
  Pallas kernels: 61.9 us -> 58.9 us
  local copies, waits for them, and re-layouts: 1.41 us -> 2.06 us
    pallas_call x2 -> x1, Pallas kernels: 61.9 us -> 58.9 us  [shards(): pl.pallas_call(kernel, name='spinners', out_shape=(field, field), in_spec...]
    unnamed x6 -> x4, local copies, waits for them, and re-layouts: 1.41 us -> 2.06 us
where the time goes in v3:
time: 61.8 us; the launch traced here: 61.6 us
  Pallas kernels  58.9 us (95%)
  local copies, waits for them, and re-layouts  2.06 us (3%)
  between operations  0.65 us (1%)
    pallas_call x1, Pallas kernels, shards(): pl.pallas_call(kernel, name='spinners', out_shape=(field, field), in_spec...  58.9 us
    unnamed x4, local copies, waits for them, and re-layouts  2.06 us

profile of v3, /device:TPU:1, one launch (start us, length us, event | category | flops | bytes accessed | tf_op | source)
XLA Modules:
  0.0 61.6 jit_solution(8871214154965545488)
XLA Ops:
  0.6 58.9 %spinners.1 = (f32[3,32,128]{2,1,0:T(8,128)}, f32[3,32,128]{2,1,0:T(8,128)}) custom-call(f32[3,32,128]{2,1,0:T(8,128)} %bitcast.8, f32[3,32,128]{2,1,0:T(8,128)} %bitcast.9, s32[2,1,16]{2,1,0:T(1,128)} %cnt.1, s32[6,2,1,16]{3,2,1,0:T(1,128)} %flg.1, bf16[8,128,128]{2,1,0:T(8,128)(2,1)} %constant.12.clone.z_far, bf16[2,256,128]{2,1,0:T(8,128)(2,1)} %constant.13.clone.lf_far, ...), custom_call_target="tpu_custom_call" | custom-call | tf_op jit(solution)/shard_map/spinners/pallas_call | solution.py:545
  59.5 0.0 copy-start
  59.5 1.4 %copy.16 = f32[3,2,1,16,128]{4,3,2,1,0:T(8,128)} copy(f32[3,2,1,16,128]{4,3,2,1,0:T(8,128)} %bitcast.11) | data formatting | bytes 98304
  60.9 0.0 copy-done
  61.0 0.6 %copy.17 = f32[3,2,1,16,128]{4,3,2,1,0:T(8,128)} copy(f32[3,2,1,16,128]{4,3,2,1,0:T(8,128)S(1)} %bitcast.10) | data formatting | bytes 98304
Async XLA Ops:
  59.5 1.4 %copy-start = (f32[3,32,128]{2,1,0:T(8,128)S(1)}, f32[3,32,128]{2,1,0:T(8,128)}, u32[]{:S(2)}) copy-start(f32[3,32,128]{2,1,0:T(8,128)} %get-tuple-element.5) | copy-start | bytes 147460

commit v4 on v3

--- a/solution.py
+++ b/solution.py
@@ -30,6 +30,7 @@
 
 A_ROWS = 32
 GROUP = SLOT // A_ROWS
+GROUPS = CELLS // GROUP
 B_ROWS = 16
 L_ROWS = 16
 A_PITCH = A_ROWS + 1
@@ -159,7 +160,7 @@
 
 def kernel(
     pos_in, tor_in, cnt, flg, z_far, lf_far, lb_far, rf_far, rb_far, twist_far, pos_out, spin,
-    near_out, state, places, gates, afeat, trans, bfeat, lfeat, totals,
+    near_out, state, places, gates, afeat, trans, bfeat, lfeat, totals, totals_z, totals_x,
     full_x, full_y, part_x, part_y, send_sem, recv_sem, tell,
     z_tab, lf, lb, rf, rb, twist, table_sem,
     grid, plan_h, plan_l, depth, out_1, in_1, out_2, in_2, work, far, all_send, all_recv, self_sem,
@@ -248,6 +249,7 @@
         afeat[pl.ds(k, CELLS, stride=A_PITCH), :] = zero
     for k in (3, 4, 5):
         afeat[pl.ds(k, CELLS, stride=A_PITCH), :] = one
+    totals_x[pl.ds(0, HALF * T_PITCH), :] = jnp.zeros((HALF * T_PITCH, SLOT), F32)
     for e in range(7):
         put(bfeat, e, 6, B_PITCH, one)
         for k in (7, 14, 15):
@@ -259,37 +261,51 @@
         blocks = [ref[e, pl.ds(cell * (n + 1), n), :] for e in faces]
         return (blocks[0] if len(blocks) == 1 else jnp.concatenate(blocks, 1)).astype(BF16)
 
-    def weighted(block, first, pairs):
+    def powers(group, faces):
+        block = trans[group]
         ats = [jnp.where(owner == k, block, jnp.zeros_like(block)) for k in range(GROUP)]
-        acc = [None] * GROUP
-        for faces in pairs:
-            b = []
-            for k in range(GROUP):
-                part = wide(bfeat, B_ROWS, first + k, faces)
-                b += [part, part]
-            b = jnp.concatenate(b, 0)
-            power = jnp.dot(jnp.concatenate(ats, 0), b, preferred_element_type=F32)
-            for k in range(GROUP):
-                w = jnp.exp2(power[k * SLOT : (k + 1) * SLOT]).astype(BF16)
-                load = wide(lfeat, L_ROWS, first + k, faces)
-                out = lax.dot_general(load, w, (((1,), (1,)), ((), ())), preferred_element_type=F32)
-                acc[k] = out if acc[k] is None else acc[k] + out
-        return acc
+        b = []
+        for k in range(GROUP):
+            part = wide(bfeat, B_ROWS, group * GROUP + k, faces)
+            b += [part, part]
+        return jnp.dot(jnp.concatenate(ats, 0), jnp.concatenate(b, 0), preferred_element_type=F32)
+
+    def add_up(load, w, side):
+        acc = lax.dot_general(load, w, (((1,), (side,)), ((), ())), preferred_element_type=F32)
+        return acc[0:8] + acc[8:16]
+
+    def inner_group(group, faces, into, power):
+        for k in range(GROUP):
+            cell = group * GROUP + k
+            w = jnp.exp2(power[k * SLOT : (k + 1) * SLOT]).astype(BF16)
+            into[pl.ds(cell * T_PITCH, 8), :] = add_up(wide(lfeat, L_ROWS, cell, faces), w, 1)
+            for n, e in enumerate(faces):
+                if e == 1:
+                    upper = (cell // HALF) * HALF + (cell + 1) % HALF
+                    load = wide(lfeat, L_ROWS, upper, (2,))
+                    totals_z[pl.ds(upper * T_PITCH, 8), :] = add_up(load, w[:, n * SLOT : (n + 1) * SLOT], 0)
+                if e == 3:
+                    load = wide(lfeat, L_ROWS, cell + HALF, (3,))
+                    totals_x[pl.ds((cell + HALF) * T_PITCH, 8), :] = add_up(load, w[:, n * SLOT : (n + 1) * SLOT], 0)
 
     def inner_faces(i, carry):
-        first = i * GROUP
-        rows = [afeat[pl.ds((first + k) * A_PITCH, A_ROWS), :] for k in range(GROUP)]
-        block = jnp.concatenate(rows, 0).T.astype(BF16)
-        trans[i] = block
-        for k, acc in enumerate(weighted(block, first, ((0, 1, 2, 3),))):
-            totals[pl.ds((first + k) * T_PITCH, 8), :] = acc[0:8] + acc[8:16]
+        low, high = powers(i, (0, 1, 3)), powers(i + GROUPS // 2, (0, 1))
+        inner_group(i, (0, 1, 3), totals, low)
+        inner_group(i + GROUPS // 2, (0, 1), totals, high)
+        for g in (i, i + GROUPS // 2):
+            turn_receivers(jnp.minimum(g + 1, GROUPS - 1))
         return carry
 
+    def turn_receivers(group):
+        rows = [afeat[pl.ds((group * GROUP + k) * A_PITCH, A_ROWS), :] for k in range(GROUP)]
+        trans[group] = jnp.concatenate(rows, 0).T.astype(BF16)
+
     def outer_faces(i, carry):
-        first = i * GROUP
-        for k, acc in enumerate(weighted(trans[i], first, ((4, 5, 6),))):
-            spot = pl.ds((first + k) * T_PITCH, 8)
-            totals[spot, :] = totals[spot, :] + (acc[0:8] + acc[8:16])
+        both = [powers(i + g * (GROUPS // 2), (4, 5, 6)) for g in range(2)]
+        for cell, power, k in [((i + g * (GROUPS // 2)) * GROUP + k, both[g], k) for g in range(2) for k in range(GROUP)]:
+            w = jnp.exp2(power[k * SLOT : (k + 1) * SLOT]).astype(BF16)
+            spot = pl.ds(cell * T_PITCH, 8)
+            totals[spot, :] = totals[spot, :] + add_up(wide(lfeat, L_ROWS, cell, (4, 5, 6)), w, 1)
         return carry
 
     for step in range(STEPS):
@@ -321,7 +337,9 @@
                 (float(CELL) if h == 0 else -float(CELL), 0.0, 0.0),
                 gates[0 if h == 0 else 1, part, :],
             )
-        lax.fori_loop(0, CELLS // GROUP, inner_faces, 0)
+        turn_receivers(0)
+        turn_receivers(GROUPS // 2)
+        lax.fori_loop(0, GROUPS // 2, inner_faces, 0)
         for copy in copies:
             copy.wait_recv()
         learn(step)
@@ -346,9 +364,12 @@
                     (0.0, float(lift), 0.0),
                     gates[face, part, :],
                 )
-        lax.fori_loop(0, CELLS // GROUP, outer_faces, 0)
-
-        tot = [totals[pl.ds(q, CELLS, stride=T_PITCH), :] for q in range(7)]
+        lax.fori_loop(0, GROUPS // 2, outer_faces, 0)
+
+        tot = []
+        for q in range(7):
+            rows = pl.ds(q, CELLS, stride=T_PITCH)
+            tot.append(totals[rows, :] + totals_z[rows, :] + totals_x[rows, :])
         fill = state[6]
         x, y, z = (here[d] for d in range(3))
         speed = (
@@ -558,6 +579,8 @@
             pltpu.VMEM((7, CELLS * B_PITCH, SLOT), F32),
             pltpu.VMEM((7, CELLS * L_PITCH, SLOT), F32),
             pltpu.VMEM((CELLS * T_PITCH, SLOT), F32),
+            pltpu.VMEM((CELLS * T_PITCH, SLOT), F32),
+            pltpu.VMEM((CELLS * T_PITCH, SLOT), F32),
             pltpu.VMEM((2, 7, HALF, SLOT), F32),
             pltpu.VMEM((2, 7, CELLS, SLOT), F32),
             pltpu.VMEM((STEPS - 1, 2, 3, HALF, SLOT), F32),

time: 61.8 us -> 58.3 us (0.943)
  Pallas kernels: 58.9 us -> 55.4 us
    pallas_call x1, Pallas kernels: 58.9 us -> 55.4 us  [shards(): pl.pallas_call(kernel, name='spinners', out_shape=(field, field), in_spec...]
where the time goes in v4:
time: 58.3 us; the launch traced here: 58.1 us
  Pallas kernels  55.4 us (95%)
  local copies, waits for them, and re-layouts  2.06 us (4%)
  between operations  0.65 us (1%)
    pallas_call x1, Pallas kernels, shards(): pl.pallas_call(kernel, name='spinners', out_shape=(field, field), in_spec...  55.4 us
    unnamed x4, local copies, waits for them, and re-layouts  2.06 us

profile of v4, /device:TPU:1, one launch (start us, length us, event | category | flops | bytes accessed | tf_op | source)
XLA Modules:
  0.0 58.1 jit_solution(1272463760701143955)
XLA Ops:
  0.6 55.4 %spinners.1 = (f32[3,32,128]{2,1,0:T(8,128)}, f32[3,32,128]{2,1,0:T(8,128)}) custom-call(f32[3,32,128]{2,1,0:T(8,128)} %bitcast.8, f32[3,32,128]{2,1,0:T(8,128)} %bitcast.9, s32[2,1,16]{2,1,0:T(1,128)} %cnt.1, s32[6,2,1,16]{3,2,1,0:T(1,128)} %flg.1, bf16[8,128,128]{2,1,0:T(8,128)(2,1)} %constant.12.clone.z_far, bf16[2,256,128]{2,1,0:T(8,128)(2,1)} %constant.13.clone.lf_far, ...), custom_call_target="tpu_custom_call" | custom-call | tf_op jit(solution)/shard_map/spinners/pallas_call | solution.py:566
  56.0 0.0 copy-start
  56.1 1.4 %copy.16 = f32[3,2,1,16,128]{4,3,2,1,0:T(8,128)} copy(f32[3,2,1,16,128]{4,3,2,1,0:T(8,128)} %bitcast.11) | data formatting | bytes 98304
  57.5 0.0 copy-done
  57.5 0.6 %copy.17 = f32[3,2,1,16,128]{4,3,2,1,0:T(8,128)} copy(f32[3,2,1,16,128]{4,3,2,1,0:T(8,128)S(1)} %bitcast.10) | data formatting | bytes 98304
Async XLA Ops:
  56.0 1.4 %copy-start = (f32[3,32,128]{2,1,0:T(8,128)S(1)}, f32[3,32,128]{2,1,0:T(8,128)}, u32[]{:S(2)}) copy-start(f32[3,32,128]{2,1,0:T(8,128)} %get-tuple-element.5) | copy-start | bytes 147460

commit v5 on v4

--- a/solution.py
+++ b/solution.py
@@ -15,6 +15,7 @@
 ROWS = 8
 COLS = 16
 DEVICES = ROWS * COLS
+BUNCH = 8
 CELLS = 32
 HALF = 16
 MESH = pl.DeviceIdType.MESH
@@ -274,26 +275,26 @@
         acc = lax.dot_general(load, w, (((1,), (side,)), ((), ())), preferred_element_type=F32)
         return acc[0:8] + acc[8:16]
 
-    def inner_group(group, faces, into, power):
-        for k in range(GROUP):
-            cell = group * GROUP + k
-            w = jnp.exp2(power[k * SLOT : (k + 1) * SLOT]).astype(BF16)
-            into[pl.ds(cell * T_PITCH, 8), :] = add_up(wide(lfeat, L_ROWS, cell, faces), w, 1)
-            for n, e in enumerate(faces):
-                if e == 1:
-                    upper = (cell // HALF) * HALF + (cell + 1) % HALF
-                    load = wide(lfeat, L_ROWS, upper, (2,))
-                    totals_z[pl.ds(upper * T_PITCH, 8), :] = add_up(load, w[:, n * SLOT : (n + 1) * SLOT], 0)
-                if e == 3:
-                    load = wide(lfeat, L_ROWS, cell + HALF, (3,))
-                    totals_x[pl.ds((cell + HALF) * T_PITCH, 8), :] = add_up(load, w[:, n * SLOT : (n + 1) * SLOT], 0)
+    def inner_cell(group, k, faces, power):
+        cell = group * GROUP + k
+        w = jnp.exp2(power[k * SLOT : (k + 1) * SLOT]).astype(BF16)
+        totals[pl.ds(cell * T_PITCH, 8), :] = add_up(wide(lfeat, L_ROWS, cell, faces), w, 1)
+        upper = (cell // HALF) * HALF + (cell + 1) % HALF
+        load = wide(lfeat, L_ROWS, upper, (2,))
+        if len(faces) == 2:
+            totals_z[pl.ds(upper * T_PITCH, 8), :] = add_up(load, w[:, SLOT:], 0)
+        else:
+            load = jnp.concatenate([load, wide(lfeat, L_ROWS, cell + HALF, (3,))], 0)
+            acc = lax.dot_general(load, w[:, SLOT:], (((1,), (0,)), ((), ())), preferred_element_type=F32)
+            totals_z[pl.ds(upper * T_PITCH, 8), :] = acc[0:8, 0:SLOT] + acc[8:16, 0:SLOT]
+            totals_x[pl.ds((cell + HALF) * T_PITCH, 8), :] = acc[16:24, SLOT:] + acc[24:32, SLOT:]
 
     def inner_faces(i, carry):
-        low, high = powers(i, (0, 1, 3)), powers(i + GROUPS // 2, (0, 1))
-        inner_group(i, (0, 1, 3), totals, low)
-        inner_group(i + GROUPS // 2, (0, 1), totals, high)
-        for g in (i, i + GROUPS // 2):
-            turn_receivers(jnp.minimum(g + 1, GROUPS - 1))
+        sides = ((i, (0, 1, 3)), (i + GROUPS // 2, (0, 1)))
+        both = [powers(g, faces) for g, faces in sides]
+        for k, n in [(k, n) for k in range(GROUP) for n in range(2)]:
+            inner_cell(sides[n][0], k, sides[n][1], both[n])
+
         return carry
 
     def turn_receivers(group):
@@ -337,8 +338,8 @@
                 (float(CELL) if h == 0 else -float(CELL), 0.0, 0.0),
                 gates[0 if h == 0 else 1, part, :],
             )
-        turn_receivers(0)
-        turn_receivers(GROUPS // 2)
+        for g in range(GROUPS):
+            turn_receivers(g)
         lax.fori_loop(0, GROUPS // 2, inner_faces, 0)
         for copy in copies:
             copy.wait_recv()
@@ -388,10 +389,6 @@
 
     me = row * COLS + col
 
-    def peer(k):
-        p = me + k
-        return jnp.where(p >= DEVICES, p - DEVICES, p)
-
     level = lax.broadcasted_iota(jnp.int32, (CELL, SLOT), 0).astype(F32) + 0.5
     low_lane = lax.broadcasted_iota(jnp.int32, (24, SLOT), 1) < 64
 
@@ -424,7 +421,7 @@
             grid[c, pl.ds(pl.multiple_of(z * 8, 8), 8), :] = block[c * 8 : c * 8 + 8]
         return carry
 
-    lax.fori_loop(0, HALF, spread, 0)
+    lax.fori_loop(0, HALF, spread, 0, unroll=4)
 
     for c in range(3):
         n = 0 if c < 2 else 2
@@ -433,8 +430,7 @@
     pl.semaphore_wait(tell.at[2], ROWS - 1)
 
     def exchange(out, into, k):
-        def post(i, carry):
-            p = peer(i)
+        def post(p):
             pltpu.make_async_remote_copy(
                 src_ref=out.at[pl.ds(pl.multiple_of(p * 8, 8), 3), :],
                 dst_ref=into.at[pl.ds(pl.multiple_of(me * 8, 8), 3), :],
@@ -443,9 +439,17 @@
                 device_id=p,
                 device_id_type=LOGICAL,
             ).start()
+
+        def post_bunch(i, carry):
+            bunch = me // BUNCH + i
+            first = jnp.where(bunch >= DEVICES // BUNCH, bunch - DEVICES // BUNCH, bunch) * BUNCH
+            for n in range(BUNCH):
+                post(first + n)
             return carry
 
-        lax.fori_loop(1, DEVICES, post, 0, unroll=9)
+        lax.fori_loop(1, DEVICES // BUNCH, post_bunch, 0)
+        for n in range(1, BUNCH):
+            post(me // BUNCH * BUNCH + lax.rem(me + n, BUNCH))
         mine = pl.ds(pl.multiple_of(me * 8, 8), 3)
         keep = pltpu.make_async_copy(out.at[mine, :], into.at[mine, :], self_sem.at[k])
         keep.start()

time: 58.3 us -> 56.7 us (0.973)
  Pallas kernels: 55.4 us -> 53.8 us
    pallas_call x1, Pallas kernels: 55.4 us -> 53.8 us  [shards(): pl.pallas_call(kernel, name='spinners', out_shape=(field, field), in_spec...]
where the time goes in v5:
time: 56.7 us; the launch traced here: 56.5 us
  Pallas kernels  53.8 us (95%)
  local copies, waits for them, and re-layouts  2.06 us (4%)
  between operations  0.65 us (1%)
    pallas_call x1, Pallas kernels, shards(): pl.pallas_call(kernel, name='spinners', out_shape=(field, field), in_spec...  53.8 us
    unnamed x4, local copies, waits for them, and re-layouts  2.06 us

profile of v5, /device:TPU:1, one launch (start us, length us, event | category | flops | bytes accessed | tf_op | source)
XLA Modules:
  0.0 56.5 jit_solution(5439520308228032012)
XLA Ops:
  0.6 53.8 %spinners.1 = (f32[3,32,128]{2,1,0:T(8,128)}, f32[3,32,128]{2,1,0:T(8,128)}) custom-call(f32[3,32,128]{2,1,0:T(8,128)} %bitcast.8, f32[3,32,128]{2,1,0:T(8,128)} %bitcast.9, s32[2,1,16]{2,1,0:T(1,128)} %cnt.1, s32[6,2,1,16]{3,2,1,0:T(1,128)} %flg.1, bf16[8,128,128]{2,1,0:T(8,128)(2,1)} %constant.12.clone.z_far, bf16[2,256,128]{2,1,0:T(8,128)(2,1)} %constant.13.clone.lf_far, ...), custom_call_target="tpu_custom_call" | custom-call | tf_op jit(solution)/shard_map/spinners/pallas_call | solution.py:570
  54.5 0.0 copy-start
  54.5 1.4 %copy.16 = f32[3,2,1,16,128]{4,3,2,1,0:T(8,128)} copy(f32[3,2,1,16,128]{4,3,2,1,0:T(8,128)} %bitcast.11) | data formatting | bytes 98304
  55.9 0.0 copy-done
  55.9 0.6 %copy.17 = f32[3,2,1,16,128]{4,3,2,1,0:T(8,128)} copy(f32[3,2,1,16,128]{4,3,2,1,0:T(8,128)S(1)} %bitcast.10) | data formatting | bytes 98304
Async XLA Ops:
  54.5 1.4 %copy-start = (f32[3,32,128]{2,1,0:T(8,128)S(1)}, f32[3,32,128]{2,1,0:T(8,128)}, u32[]{:S(2)}) copy-start(f32[3,32,128]{2,1,0:T(8,128)} %get-tuple-element.5) | copy-start | bytes 147460

commit v6 on v5

--- a/solution.py
+++ b/solution.py
@@ -90,14 +90,21 @@
     return lax.dot_general(a, b, (((1,), (1,)), ((), ())), preferred_element_type=F32)
 
 
-def table_left(high, low, v):
+def table_left(table, v):
     vh, vl = cut(v)
-    return mul(high, vh) + (mul(low, vh) + mul(high, vl))
-
-
-def table_right(v, high, low):
-    vh, vl = cut(v)
-    return mul(vh, high) + (mul(vl, high) + mul(vh, low))
+    rows = table.shape[1]
+    both = mul(table.reshape(2 * rows, table.shape[2]), vh)
+    return both[:rows] + (both[rows:] + mul(table[0], vl))
+
+
+def table_right(parts, table):
+    cuts = [cut(v) for v in parts]
+    high = jnp.concatenate([h for h, _ in cuts], 0)
+    both = mul(jnp.concatenate([high] + [l for _, l in cuts], 0), table[0])
+    rows = high.shape[0]
+    total = both[:rows] + (both[rows:] + mul(high, table[1]))
+    size = parts[0].shape[0]
+    return [total[n * size : (n + 1) * size] for n in range(len(parts))]
 
 
 def narrow(v):
@@ -134,18 +141,19 @@
     row(16 + 6, size[1])
 
 
-def put_source(bfeat, lfeat, slot, half, place, torque, fill, shift, gate):
+def put_source(bfeat, lfeat, slot, half, place, torque, fill, shift, gate, loads_only=False):
     place = [place[d] + shift[d] if shift[d] != 0.0 else place[d] for d in range(3)]
     x, y, z = place
-    base = half * HALF * B_PITCH
-    for d in range(3):
-        h, m, l = split3(place[d])
-        put(bfeat, slot, base + d, B_PITCH, h)
-        put(bfeat, slot, base + 8 + d, B_PITCH, m)
-        put(bfeat, slot, base + 11 + d, B_PITCH, l)
-        put(bfeat, slot, base + (7, 14, 15)[d], B_PITCH, h)
-    for k, v in enumerate(split3(-KAPPA * (x * x + y * y + z * z))):
-        put(bfeat, slot, base + 3 + k, B_PITCH, v)
+    if not loads_only:
+        base = half * HALF * B_PITCH
+        for d in range(3):
+            h, m, l = split3(place[d])
+            put(bfeat, slot, base + d, B_PITCH, h)
+            put(bfeat, slot, base + 8 + d, B_PITCH, m)
+            put(bfeat, slot, base + 11 + d, B_PITCH, l)
+            put(bfeat, slot, base + (7, 14, 15)[d], B_PITCH, h)
+        for k, v in enumerate(split3(-KAPPA * (x * x + y * y + z * z))):
+            put(bfeat, slot, base + 3 + k, B_PITCH, v)
     if gate is not None:
         torque = [t * gate for t in torque]
         fill = fill * gate
@@ -160,8 +168,8 @@
 
 
 def kernel(
-    pos_in, tor_in, cnt, flg, z_far, lf_far, lb_far, rf_far, rb_far, twist_far, pos_out, spin,
-    near_out, state, places, gates, afeat, trans, bfeat, lfeat, totals, totals_z, totals_x,
+    pos_far, tor_far, cnt_far, flg_far, z_far, lf_far, lb_far, rf_far, rb_far, twist_far, moved_far, spin,
+    pos_in, tor_in, pos_out, cnt, flg, field_sem, near_out, state, places, gates, afeat, trans, bfeat, lfeat, totals, totals_z, totals_x,
     full_x, full_y, part_x, part_y, send_sem, recv_sem, tell,
     z_tab, lf, lb, rf, rb, twist, table_sem,
     grid, plan_h, plan_l, depth, out_1, in_1, out_2, in_2, work, far, all_send, all_recv, self_sem,
@@ -178,6 +186,12 @@
     for peer in peers:
         pl.semaphore_signal(barrier, inc=1, device_id=peer, device_id_type=MESH)
 
+    fields = [
+        pltpu.make_async_copy(src, dst, field_sem.at[k])
+        for k, (src, dst) in enumerate(((pos_far, pos_in), (tor_far, tor_in), (cnt_far, cnt), (flg_far, flg)))
+    ]
+    for field in fields:
+        field.start()
     tables = [
         pltpu.make_async_copy(src, dst, table_sem.at[k])
         for k, (src, dst) in enumerate(
@@ -211,6 +225,8 @@
                 gates[f, pl.ds(h * HALF + z, 1), :] = jnp.full((1, SLOT), flg[f, h, 0, z], jnp.int32).astype(F32)
         return carry
 
+    for field in fields:
+        field.wait()
     lax.fori_loop(0, HALF, spread_scalars, 0)
     fill = state[6]
     for d in range(3):
@@ -328,7 +344,7 @@
 
                 put_source(
                     bfeat, lfeat, slot, h, [turned(v) for v in place], [turned(v) for v in torque], turned(fill),
-                    (0.0, 0.0, float(lift)), gates[face, part, :],
+                    (0.0, 0.0, float(lift)), gates[face, part, :], loads_only=slot == 2,
                 )
             put_source(
                 bfeat, lfeat, 3, h,
@@ -337,6 +353,7 @@
                 state[6, other, :],
                 (float(CELL) if h == 0 else -float(CELL), 0.0, 0.0),
                 gates[0 if h == 0 else 1, part, :],
+                loads_only=h == 1,
             )
         for g in range(GROUPS):
             turn_receivers(g)
@@ -392,6 +409,8 @@
     level = lax.broadcasted_iota(jnp.int32, (CELL, SLOT), 0).astype(F32) + 0.5
     low_lane = lax.broadcasted_iota(jnp.int32, (24, SLOT), 1) < 64
 
+    give = pltpu.make_async_copy(pos_out, moved_far, field_sem.at[4])
+    give.start()
     for table in tables:
         table.wait()
 
@@ -423,9 +442,12 @@
 
     lax.fori_loop(0, HALF, spread, 0, unroll=4)
 
-    for c in range(3):
-        n = 0 if c < 2 else 2
-        out_1[pl.ds(c, DEVICES, stride=8), :] = table_left(z_tab[n], z_tab[n + 1], grid[c])
+    def along_z(first, v):
+        pair = table_left(z_tab[first : first + 2], jnp.concatenate(v[0:2], 1))
+        return pair[:, 0:128], pair[:, 128:256], table_left(z_tab[first + 2 : first + 4], v[2])
+
+    for c, v in enumerate(along_z(0, [grid[c] for c in range(3)])):
+        out_1[pl.ds(c, DEVICES, stride=8), :] = v
 
     pl.semaphore_wait(tell.at[2], ROWS - 1)
 
@@ -460,13 +482,14 @@
     exchange(out_1, in_1, 0)
 
     cos_t, sin_t = twist[0], twist[1]
+    planes = jnp.concatenate([in_1[pl.ds(c, DEVICES, stride=8), :] for c in range(3)], 1)
+    both = table_left(lf[...], planes)
+    turned = []
     for c in range(3):
-        both = table_left(lf[0], lf[1], in_1[pl.ds(c, DEVICES, stride=8), :])
-        re, im = both[0:128], both[128:256]
-        work[c, :, 0:128] = re * cos_t + im * sin_t
-        work[c, :, 128:256] = im * cos_t - re * sin_t
-    for c in range(3):
-        work[c] = table_right(work[c], rf[0], rf[1])
+        re, im = both[0:128, c * 128 : c * 128 + 128], both[128:256, c * 128 : c * 128 + 128]
+        turned.append(jnp.concatenate([re * cos_t + im * sin_t, im * cos_t - re * sin_t], 1))
+    for c, v in enumerate(table_right(turned, rf)):
+        work[c] = v
 
     special = me < 2
     plain = jnp.where(special, 1.0, 0.0).astype(F32)
@@ -516,17 +539,18 @@
 
     lax.fori_loop(0, 8, stokes, 0)
 
+    pairs = []
+    for both in table_right([work[c] for c in range(3)], rb):
+        re, im = both[:, 0:128], both[:, 128:256]
+        pairs.append(jnp.concatenate([re * cos_t - im * sin_t, im * cos_t + re * sin_t], 0))
+    planes = table_left(lb[...], jnp.concatenate(pairs, 1))
     for c in range(3):
-        both = table_right(work[c], rb[0], rb[1])
-        re, im = both[:, 0:128], both[:, 128:256]
-        pair = jnp.concatenate([re * cos_t - im * sin_t, im * cos_t + re * sin_t], 0)
-        out_2[pl.ds(c, DEVICES, stride=8), :] = table_left(lb[0], lb[1], pair)
+        out_2[pl.ds(c, DEVICES, stride=8), :] = planes[:, c * 128 : c * 128 + 128]
 
     exchange(out_2, in_2, 1)
 
-    for c in range(3):
-        n = 4 if c < 2 else 6
-        grid[c] = table_left(z_tab[n], z_tab[n + 1], in_2[pl.ds(c, DEVICES, stride=8), :])
+    for c, v in enumerate(along_z(4, [in_2[pl.ds(c, DEVICES, stride=8), :] for c in range(3)])):
+        grid[c] = v
 
     def gather(z, carry):
         rows = pl.ds(pl.multiple_of(z * 8, 8), 8)
@@ -556,6 +580,7 @@
     for k in range(2):
         bulk = out_1.at[pl.ds(0, 3 * (DEVICES - 1)), :]
         pltpu.make_async_copy(bulk, bulk, all_send.at[k]).wait()
+    give.wait()
     for step in range(STEPS):
         for copy in halo(step):
             copy.wait_send()
@@ -564,16 +589,22 @@
     flat = (3, CELLS, SLOT)
     tables = [jnp.asarray(t) for t in make_tables()]
     vmem = pl.BlockSpec(memory_space=pltpu.VMEM)
-    smem = pl.BlockSpec(memory_space=pltpu.SMEM)
+    there = pl.BlockSpec(memory_space=pl.ANY)
     field = jax.ShapeDtypeStruct(flat, F32)
     buffer = pltpu.VMEM((DEVICES * 8, 128), F32)
     places, spin = pl.pallas_call(
         kernel,
         name="spinners",
         out_shape=(field, field),
-        in_specs=[vmem, vmem, smem, smem] + [pl.BlockSpec(memory_space=pl.ANY)] * len(tables),
-        out_specs=(vmem, vmem),
+        in_specs=[there] * (4 + len(tables)),
+        out_specs=(there, vmem),
         scratch_shapes=[
+            pltpu.VMEM(flat, F32),
+            pltpu.VMEM(flat, F32),
+            pltpu.VMEM(flat, F32),
+            pltpu.SMEM(counts.shape, jnp.int32),
+            pltpu.SMEM(neighbour_flags.shape, jnp.int32),
+            pltpu.SemaphoreType.DMA((5,)),
             pltpu.VMEM(flat, F32),
             pltpu.VMEM((7, CELLS, SLOT), F32),
             pltpu.VMEM((STEPS - 1, 3, CELLS, SLOT), F32),

time: 56.7 us -> 55.8 us (0.984)
  Pallas kernels: 53.8 us -> 52.9 us
    pallas_call x1, Pallas kernels: 53.8 us -> 52.9 us  [shards(): pl.pallas_call(kernel, name='spinners', out_shape=(field, field), in_spec...]
where the time goes in v6:
time: 55.8 us; the launch traced here: 55.6 us
  Pallas kernels  52.9 us (95%)
  local copies, waits for them, and re-layouts  2.06 us (4%)
  between operations  0.65 us (1%)
    pallas_call x1, Pallas kernels, shards(): pl.pallas_call(kernel, name='spinners', out_shape=(field, field), in_spec...  52.9 us
    unnamed x4, local copies, waits for them, and re-layouts  2.06 us

profile of v6, /device:TPU:1, one launch (start us, length us, event | category | flops | bytes accessed | tf_op | source)
XLA Modules:
  0.0 55.6 jit_solution(16771530063620065734)
XLA Ops:
  0.6 52.9 %spinners.1 = (f32[3,32,128]{2,1,0:T(8,128)}, f32[3,32,128]{2,1,0:T(8,128)}) custom-call(f32[3,32,128]{2,1,0:T(8,128)} %bitcast.8, f32[3,32,128]{2,1,0:T(8,128)} %bitcast.9, s32[2,1,16]{2,1,0:T(1,128)} %cnt_far.1, s32[6,2,1,16]{3,2,1,0:T(1,128)} %flg_far.1, bf16[8,128,128]{2,1,0:T(8,128)(2,1)} %constant.12.clone.z_far, ...), custom_call_target="tpu_custom_call" | custom-call | tf_op jit(solution)/shard_map/spinners/pallas_call | solution.py:595
  53.6 0.0 copy-start
  53.6 1.4 %copy.16 = f32[3,2,1,16,128]{4,3,2,1,0:T(8,128)} copy(f32[3,2,1,16,128]{4,3,2,1,0:T(8,128)} %bitcast.11) | data formatting | bytes 98304
  55.0 0.0 copy-done
  55.0 0.6 %copy.17 = f32[3,2,1,16,128]{4,3,2,1,0:T(8,128)} copy(f32[3,2,1,16,128]{4,3,2,1,0:T(8,128)S(1)} %bitcast.10) | data formatting | bytes 98304
Async XLA Ops:
  53.6 1.4 %copy-start = (f32[3,32,128]{2,1,0:T(8,128)S(1)}, f32[3,32,128]{2,1,0:T(8,128)}, u32[]{:S(2)}) copy-start(f32[3,32,128]{2,1,0:T(8,128)} %get-tuple-element.5) | copy-start | bytes 147460

commit v7 on v6

--- a/solution.py
+++ b/solution.py
@@ -168,8 +168,8 @@
 
 
 def kernel(
-    pos_far, tor_far, cnt_far, flg_far, z_far, lf_far, lb_far, rf_far, rb_far, twist_far, moved_far, spin,
-    pos_in, tor_in, pos_out, cnt, flg, field_sem, near_out, state, places, gates, afeat, trans, bfeat, lfeat, totals, totals_z, totals_x,
+    pos_far, tor_far, cnt_far, flg_far, z_far, lf_far, lb_far, rf_far, rb_far, twist_far, out_far,
+    pos_in, tor_in, pos_out, spin, cnt, flg, field_sem, near_out, state, places, gates, afeat, trans, bfeat, lfeat, totals, totals_z, totals_x,
     full_x, full_y, part_x, part_y, send_sem, recv_sem, tell,
     z_tab, lf, lb, rf, rb, twist, table_sem,
     grid, plan_h, plan_l, depth, out_1, in_1, out_2, in_2, work, far, all_send, all_recv, self_sem,
@@ -400,7 +400,7 @@
             if step < STEPS - 1:
                 places[step, d] = moved
             else:
-                pos_out[d] = moved + MID
+                pos_out[d] = moved
                 torque = tor_in[d]
                 near_out[d] = (torque + COUPLE * (tot[d] - tot[6] * torque)) * fill
 
@@ -409,13 +409,14 @@
     level = lax.broadcasted_iota(jnp.int32, (CELL, SLOT), 0).astype(F32) + 0.5
     low_lane = lax.broadcasted_iota(jnp.int32, (24, SLOT), 1) < 64
 
-    give = pltpu.make_async_copy(pos_out, moved_far, field_sem.at[4])
-    give.start()
+    gives = [pltpu.make_async_copy(src, out_far.at[k], field_sem.at[4 + k]) for k, src in enumerate((pos_out, near_out, spin))]
+    for give in gives[0:2]:
+        give.start()
     for table in tables:
         table.wait()
 
     def bins(d, cell):
-        apart = pos_out[d, pl.ds(cell, 1), :] - level
+        apart = pos_out[d, pl.ds(cell, 1), :] + MID - level
         return jnp.exp(-apart * apart)
 
     def spread(z, carry):
@@ -575,12 +576,14 @@
         total = far[c, pl.ds(0, CELLS, stride=8), :]
         for g in range(1, CELL):
             total = total + far[c, pl.ds(g, CELLS, stride=8), :]
-        spin[c] = near_out[c] + total * state[6]
+        spin[c] = total * state[6]
+    gives[2].start()
 
     for k in range(2):
         bulk = out_1.at[pl.ds(0, 3 * (DEVICES - 1)), :]
         pltpu.make_async_copy(bulk, bulk, all_send.at[k]).wait()
-    give.wait()
+    for give in gives:
+        give.wait()
     for step in range(STEPS):
         for copy in halo(step):
             copy.wait_send()
@@ -588,23 +591,22 @@
     shape = positions.shape
     flat = (3, CELLS, SLOT)
     tables = [jnp.asarray(t) for t in make_tables()]
-    vmem = pl.BlockSpec(memory_space=pltpu.VMEM)
     there = pl.BlockSpec(memory_space=pl.ANY)
-    field = jax.ShapeDtypeStruct(flat, F32)
     buffer = pltpu.VMEM((DEVICES * 8, 128), F32)
-    places, spin = pl.pallas_call(
+    out = pl.pallas_call(
         kernel,
         name="spinners",
-        out_shape=(field, field),
+        out_shape=jax.ShapeDtypeStruct((3,) + flat, F32),
         in_specs=[there] * (4 + len(tables)),
-        out_specs=(there, vmem),
+        out_specs=there,
         scratch_shapes=[
+            pltpu.VMEM(flat, F32),
             pltpu.VMEM(flat, F32),
             pltpu.VMEM(flat, F32),
             pltpu.VMEM(flat, F32),
             pltpu.SMEM(counts.shape, jnp.int32),
             pltpu.SMEM(neighbour_flags.shape, jnp.int32),
-            pltpu.SemaphoreType.DMA((5,)),
+            pltpu.SemaphoreType.DMA((7,)),
             pltpu.VMEM(flat, F32),
             pltpu.VMEM((7, CELLS, SLOT), F32),
             pltpu.VMEM((STEPS - 1, 3, CELLS, SLOT), F32),
@@ -643,7 +645,7 @@
         ],
         compiler_params=pltpu.CompilerParams(collective_id=0, has_side_effects=True),
     )(positions.reshape(flat), torques.reshape(flat), counts, neighbour_flags, *tables)
-    return places.reshape(shape), spin.reshape(shape)
+    return (out[0] + MID).reshape(shape), (out[1] + out[2]).reshape(shape)
 
 
 def solution(mesh):

time: 55.8 us -> 55.2 us (0.989)
  local copies, waits for them, and re-layouts: 2.06 us -> 0 us
  other arithmetic: 0 us -> 1.49 us
    unnamed x4 -> x0, local copies, waits for them, and re-layouts: 2.06 us -> none
    add x0 -> x1, other arithmetic: none -> 1.49 us  [shards(): return ((out[0] + MID).reshape(shape), (out[1] + out[2]).reshape(shape))]
where the time goes in v7:
time: 55.2 us; the launch traced here: 55.1 us
  Pallas kernels  52.9 us (96%)
  other arithmetic  1.49 us (3%)
  between operations  0.64 us (1%)
    pallas_call x1, Pallas kernels, shards(): pl.pallas_call(kernel, name='spinners', out_shape=jax.ShapeDtypeStruct((3...  52.9 us
    add x1, other arithmetic, shards(): return ((out[0] + MID).reshape(shape), (out[1] + out[2]).reshape(shape))  1.49 us

profile of v7, /device:TPU:1, one launch (start us, length us, event | category | flops | bytes accessed | tf_op | source)
XLA Modules:
  0.0 55.1 jit_solution(16364224494882567046)
XLA Ops:
  0.6 52.9 %spinners.1 = f32[3,3,32,128]{3,2,1,0:T(8,128)} custom-call(f32[3,32,128]{2,1,0:T(8,128)} %bitcast.8, f32[3,32,128]{2,1,0:T(8,128)} %bitcast.9, s32[2,1,16]{2,1,0:T(1,128)} %cnt_far.1, s32[6,2,1,16]{3,2,1,0:T(1,128)} %flg_far.1, bf16[8,128,128]{2,1,0:T(8,128)(2,1)} %constant.14.clone.z_far, bf16[2,256,128]{2,1,0:T(8,128)(2,1)} %constant.15.clone.lf_far, ...), custom_call_target="tpu_custom_call" | custom-call | tf_op jit(solution)/shard_map/spinners/pallas_call | solution.py:596
  53.6 1.5 %slice_add_fusion = (f32[1,3,32,128]{3,2,1,0:T(8,128)}, f32[1,3,32,128]{3,2,1,0:T(8,128)}) fusion(f32[3,3,32,128]{3,2,1,0:T(8,128)} %spinners.1), kind=kLoop, calls=%fused_computation | loop fusion | flops 24576 | bytes 245760 | tf_op jit(solution)/shard_map/add | solution.py:648
